TPU v7x, 32 devices: a whole 2x2x4 slice. The times are simulated.
32 devices in a mesh: row: 2 (over y), col: 16 (over z, x, core).
Axes of the slice: x: 2, y: 2, z: 4, core: 2. Of those that a mesh axis runs over, the one named last changes fastest.
Arguments:
- queries: bfloat16 [8192, 1024], P(('row', 'col')), may hold values from -8 to 8
- key_rows: bfloat16 [8192, 1024], P(('row', 'col')), may hold values from -8 to 8
- value_rows: bfloat16 [8192, 1024], P(('row', 'col')), may hold values from -6 to 6
- out_grad: bfloat16 [8192, 1024], P(('row', 'col')), may hold values from -6 to 6
- dropout_bits: int32 [8192, 128], P(('row', 'col')), may hold values from 0 to 255, as said below
- partner: int32 [3, 2, 16], replicated, may hold values from 0 to 15, each once within a row
- block_pick: int32 [3, 2, 16], replicated, may hold values from 0 to 1
- global_blocks: int32 [2], replicated, may hold values from 0 to 63
Outputs:
- attended: bfloat16 [8192, 1024], P(('row', 'col'))
- query_grad: bfloat16 [8192, 1024], P(('row', 'col'))
- key_grad: bfloat16 [8192, 1024], P(('row', 'col'))
- value_grad: bfloat16 [8192, 1024], P(('row', 'col'))
Inputs may be any that keep to these rules, and one draw needn't show every extreme that they name: `dropout_bits`: each word packs 8 flags of 0 or 1 in its low bits. partner[r, a, :] is a permutation of the places 0 to 15.
All inputs are finite; a program needn't handle non-finite values.
Results may differ from a plain program's by a relative error of at most 0.0085.
Values may be sent and summed in bfloat16 or wider, within the bound.
A program may use at most 128 MiB of HBM per device.

v0:
```python
import jax
import jax.numpy as jnp
from jax import lax
from jax.sharding import PartitionSpec as P

HEADS = 16
HEAD_DIM = 64
BLOCK = 128
NGLOBAL = 2
NMATCH = 3


score_scale = 0.125
keep_scale = 1.0 / 0.9


def extended_2(value, sides, width):
    for axis, dim in sides:
        size, length = (lax.axis_size(axis), value.shape[dim])
        up = [(i, (i + 1) % size) for i in range(size)]
        down = [(j, i) for i, j in up]
        last = lax.slice_in_dim(value, length - width, length, axis=dim)
        leading = lax.slice_in_dim(value, 0, width, axis=dim)
        before = lax.ppermute(last, axis, up)
        after = lax.ppermute(leading, axis, down)
        value = jnp.concatenate([before, value, after], axis=dim)
    return value


def spread(value, axis, root):
    mine = lax.axis_index(axis) == root
    return lax.psum(jnp.where(mine, value, jnp.zeros_like(value)), axis)


def unpack_bits(packed):
    shifts = jnp.arange(8, dtype=jnp.int32)
    flags = jnp.right_shift(packed[..., None], shifts) & 1
    return flags.reshape(packed.shape[:-1] + (packed.shape[-1] * 8,))


def split_heads(array, lower, upper, group_heads):
    part_cols = array[..., lower:upper]
    return part_cols.reshape(
        part_cols.shape[:-1] + (group_heads, part_cols.shape[-1] // group_heads)
    )


def route_blocks(pieces_in, ordering):
    total_cols = lax.axis_size("col")
    matched, rows_in, channels = pieces_in.shape
    split_rows = pieces_in.reshape(matched, total_cols, rows_in // total_cols, channels)
    spread_out = lax.all_to_all(split_rows, "col", split_axis=1, concat_axis=1, tiled=True)
    arranged = jnp.stack([spread_out[matching][ordering[matching]] for matching in range(matched)])
    arrived = lax.all_to_all(arranged, "col", split_axis=1, concat_axis=1, tiled=True)
    return arrived.reshape(matched, rows_in, channels)


def route_all(pieces_in, ordering):
    return route_blocks(pieces_in, ordering)


def body(queries, key_rows, value_rows, out_grad, dropout_bits, partner, block_pick, global_blocks):
    tokens_here, model_width = queries.shape
    blocks_here = tokens_here // BLOCK
    group_heads = min(4, HEADS)
    group_width = group_heads * HEAD_DIM
    near_rows = 3 * BLOCK
    both_rows = jnp.concatenate([key_rows, value_rows], 1)
    band_index = lax.axis_index("row")
    place_index = lax.axis_index("col")
    total_cols = lax.axis_size("col")
    segment = band_index * total_cols + place_index
    extended = extended_2(both_rows, ((("row", "col"), 0),), BLOCK)
    shared_parts = []
    for global_slot in range(NGLOBAL):
        position = global_blocks[global_slot]
        source_piece = lax.dynamic_slice_in_dim(both_rows, position % blocks_here * BLOCK, BLOCK, 0)
        shared_parts.append(spread(source_piece, ("row", "col"), position // blocks_here))
    ordering = lax.dynamic_index_in_dim(partner, band_index, 1, keepdims=False)
    picks_row = lax.dynamic_index_in_dim(block_pick, band_index, 1, keepdims=False)
    col_ids = jnp.arange(total_cols, dtype=jnp.int32)
    inverse = jnp.sum(
        jnp.where(ordering[:, :, None] == col_ids[None, None, :], col_ids[None, :, None], 0), axis=1
    )
    askers = lax.dynamic_index_in_dim(inverse, place_index, 1, keepdims=False)
    wanted = jnp.take_along_axis(picks_row, askers[:, None], axis=1)[:, 0]
    outgoing = jnp.stack(
        [
            lax.dynamic_slice_in_dim(both_rows, wanted[matching] * BLOCK, BLOCK, 0)
            for matching in range(NMATCH)
        ]
    )
    fetched = route_all(outgoing, ordering)
    shared = jnp.concatenate(shared_parts + [fetched.reshape(NMATCH * BLOCK, 2 * model_width)], 0)
    windows = jnp.stack(
        [
            extended[start_block * BLOCK : start_block * BLOCK + near_rows]
            for start_block in range(blocks_here)
        ]
    )
    keep_mask = (unpack_bits(dropout_bits).astype(jnp.float32) * keep_scale).reshape(
        blocks_here, BLOCK, -1
    )
    keep_near = keep_mask[..., :near_rows][:, None]
    keep_far = keep_mask[..., near_rows:][:, None]
    query_blocks = queries.reshape(blocks_here, BLOCK, model_width)
    grad_blocks = out_grad.reshape(blocks_here, BLOCK, model_width)
    out_parts, query_parts = ([], [])
    key_near_parts, value_near_parts, key_far_parts, value_far_parts = ([], [], [], [])
    for group_index in range(HEADS // group_heads):
        lower = group_index * group_width
        upper = lower + group_width
        query_group = split_heads(query_blocks, lower, upper, group_heads)
        grad_group = split_heads(grad_blocks, lower, upper, group_heads)
        keys_near = split_heads(windows, lower, upper, group_heads)
        values_near = split_heads(windows, model_width + lower, model_width + upper, group_heads)
        keys_far = split_heads(shared, lower, upper, group_heads)
        values_far = split_heads(shared, model_width + lower, model_width + upper, group_heads)
        score_near = (
            jnp.einsum(
                "jqgd,jkgd->jgqk", query_group, keys_near, preferred_element_type=jnp.float32
            )
            * score_scale
        )
        score_far = (
            jnp.einsum("jqgd,kgd->jgqk", query_group, keys_far, preferred_element_type=jnp.float32)
            * score_scale
        )
        top = jnp.maximum(
            jnp.max(score_near, -1, keepdims=True), jnp.max(score_far, -1, keepdims=True)
        )
        total = jnp.sum(jnp.exp(score_near - top), -1, keepdims=True) + jnp.sum(
            jnp.exp(score_far - top), -1, keepdims=True
        )
        log_total = top + jnp.log(total)
        probs_near = jnp.exp(score_near - log_total)
        probs_far = jnp.exp(score_far - log_total)
        dropped_near = (probs_near * keep_near).astype(jnp.bfloat16)
        dropped_far = (probs_far * keep_far).astype(jnp.bfloat16)
        output_group = jnp.einsum(
            "jgqk,jkgd->jqgd", dropped_near, values_near, preferred_element_type=jnp.float32
        ) + jnp.einsum(
            "jgqk,kgd->jqgd", dropped_far, values_far, preferred_element_type=jnp.float32
        )
        out_parts.append(output_group.reshape(blocks_here, BLOCK, group_width))
        grad_near = (
            jnp.einsum(
                "jqgd,jkgd->jgqk", grad_group, values_near, preferred_element_type=jnp.float32
            )
            * keep_near
        )
        grad_far = (
            jnp.einsum("jqgd,kgd->jgqk", grad_group, values_far, preferred_element_type=jnp.float32)
            * keep_far
        )
        delta = jnp.sum(probs_near * grad_near, -1, keepdims=True) + jnp.sum(
            probs_far * grad_far, -1, keepdims=True
        )
        dscore_near = (probs_near * (grad_near - delta)).astype(jnp.bfloat16)
        dscore_far = (probs_far * (grad_far - delta)).astype(jnp.bfloat16)
        query_group_grad = score_scale * (
            jnp.einsum(
                "jgqk,jkgd->jqgd", dscore_near, keys_near, preferred_element_type=jnp.float32
            )
            + jnp.einsum("jgqk,kgd->jqgd", dscore_far, keys_far, preferred_element_type=jnp.float32)
        )
        query_parts.append(query_group_grad.reshape(blocks_here, BLOCK, group_width))
        key_near_parts.append(
            (
                score_scale
                * jnp.einsum(
                    "jgqk,jqgd->jkgd", dscore_near, query_group, preferred_element_type=jnp.float32
                )
            ).reshape(blocks_here, near_rows, group_width)
        )
        value_near_parts.append(
            jnp.einsum(
                "jgqk,jqgd->jkgd", dropped_near, grad_group, preferred_element_type=jnp.float32
            ).reshape(blocks_here, near_rows, group_width)
        )
        key_far_parts.append(
            (
                score_scale
                * jnp.einsum(
                    "jgqk,jqgd->kgd", dscore_far, query_group, preferred_element_type=jnp.float32
                )
            ).reshape(-1, group_width)
        )
        value_far_parts.append(
            jnp.einsum(
                "jgqk,jqgd->kgd", dropped_far, grad_group, preferred_element_type=jnp.float32
            ).reshape(-1, group_width)
        )
    attended = jnp.concatenate(out_parts, -1).astype(jnp.bfloat16).reshape(tokens_here, model_width)
    query_grad = (
        jnp.concatenate(query_parts, -1).astype(jnp.bfloat16).reshape(tokens_here, model_width)
    )
    near_grads = jnp.concatenate(key_near_parts + value_near_parts, -1)
    far_grads = jnp.concatenate(key_far_parts + value_far_parts, -1)
    window_total = jnp.zeros((tokens_here + 2 * BLOCK, 2 * model_width), jnp.float32)
    for start_block in range(blocks_here):
        window_total = window_total.at[start_block * BLOCK : start_block * BLOCK + near_rows].add(
            near_grads[start_block]
        )
    rims = jnp.concatenate([window_total[:BLOCK], window_total[-BLOCK:]], 0).astype(jnp.bfloat16)
    returned = extended_2(rims, ((("row", "col"), 0),), BLOCK)
    gradients = window_total[BLOCK : BLOCK + tokens_here]
    gradients = gradients.at[:BLOCK].add(returned[:BLOCK].astype(jnp.float32))
    gradients = gradients.at[tokens_here - BLOCK :].add(returned[3 * BLOCK :].astype(jnp.float32))
    global_sum = lax.psum(far_grads[: NGLOBAL * BLOCK], ("row", "col"))
    for global_slot in range(NGLOBAL):
        position = global_blocks[global_slot]
        owner_here = position // blocks_here == segment
        row_offset = position % blocks_here * BLOCK
        current = lax.dynamic_slice_in_dim(gradients, row_offset, BLOCK, 0)
        addition = jnp.where(
            owner_here, global_sum[global_slot * BLOCK : (global_slot + 1) * BLOCK], 0.0
        )
        gradients = lax.dynamic_update_slice_in_dim(gradients, current + addition, row_offset, 0)
    random_grads = (
        far_grads[NGLOBAL * BLOCK :].reshape(NMATCH, BLOCK, 2 * model_width).astype(jnp.bfloat16)
    )
    came_back = route_all(random_grads, inverse)
    for matching in range(NMATCH):
        row_offset = wanted[matching] * BLOCK
        current = lax.dynamic_slice_in_dim(gradients, row_offset, BLOCK, 0)
        gradients = lax.dynamic_update_slice_in_dim(
            gradients, current + came_back[matching].astype(jnp.float32), row_offset, 0
        )
    return (
        attended,
        query_grad,
        gradients[:, :model_width].astype(jnp.bfloat16),
        gradients[:, model_width:].astype(jnp.bfloat16),
    )


def solution(mesh):
    in_specs = (
        P(("row", "col"), None),
        P(("row", "col"), None),
        P(("row", "col"), None),
        P(("row", "col"), None),
        P(("row", "col"), None),
        P(),
        P(),
        P(),
    )
    out_specs = (
        P(("row", "col"), None),
        P(("row", "col"), None),
        P(("row", "col"), None),
        P(("row", "col"), None),
    )
    return jax.shard_map(body, mesh=mesh, in_specs=in_specs, out_specs=out_specs, check_vma=False)
```

profile of v0, /device:TPU:9, one launch (start us, length us, event | category | flops | bytes accessed | tf_op | source)
XLA Modules:
  0.0 562.6 jit_solution(7647314221902579277)
XLA Ops:
  22.5 6.7 %all-to-all-start = ((bf16[3,16,8,2048]{3,2,0,1:T(8,128)(2,1)}), bf16[3,16,8,2048]{3,2,0,1:T(8,128)(2,1)S(1)}, u32[]{:S(2)}, u32[]{:S(2)}) async-start(bf16[3,16,8,2048]{3,2,0,1:T(8,128)(2,1)} %pad_maximum_fusion.1), calls=%async_computation | async-start | bytes 3145728 | tf_op jit(solution)/shard_map/all_to_all | solution.py:52
  29.3 35.5 %all-to-all-done = bf16[3,16,8,2048]{3,2,0,1:T(8,128)(2,1)S(1)} async-done(((bf16[3,16,8,2048]{3,2,0,1:T(8,128)(2,1)}), bf16[3,16,8,2048]{3,2,0,1:T(8,128)(2,1)S(1)}, u32[]{:S(2)}, u32[]{:S(2)}) %all-to-all-start) | async-done | bytes 1572896 | tf_op jit(solution)/shard_map/all_to_all | solution.py:52
  65.9 1.6 gather_fusion
  67.5 1.6 gather_fusion.1
  71.2 5.5 all-to-all-start.1
  79.2 3.5 convert_multiply_fusion
  92.3 3.3 collective-permute-done.1
  98.3 1.9 copy.741
  105.6 1.6 bitcast_reduce_fusion.5
  109.4 12.8 %all-to-all-done.1 = bf16[3,16,8,2048]{3,2,0,1:T(8,128)(2,1)} async-done(((bf16[3,16,8,2048]{3,2,0,1:T(8,128)(2,1)}), bf16[3,16,8,2048]{3,2,0,1:T(8,128)(2,1)}, u32[]{:S(2)}, u32[]{:S(2)}) %all-to-all-start.1) | async-done | bytes 1572896 | tf_op jit(solution)/shard_map/all_to_all | solution.py:54
  122.1 2.7 copy.751
  124.9 101.0 %all-reduce.7.cloned.1.call-done = (bf16[128,2048]{1,0:T(8,128)(2,1)}, bf16[128,2048]{1,0:T(8,128)(2,1)}) async-done(((bf16[128,2048]{1,0:T(8,128)(2,1)}, bf16[128,2048]{1,0:T(8,128)(2,1)}), (bf16[128,2048]{1,0:T(8,128)(2,1)}, bf16[128,2048]{1,0:T(8,128)(2,1)})) %all-reduce.7.cloned.1.call-update) | async-done | bytes 1048592 | tf_op jit(solution)/shard_map/psum | solution.py:32
  225.9 2.0 pad_maximum_fusion
  229.4 1.9 copy.752
  231.3 1.9 copy.800
  233.2 1.9 copy.794
  235.1 1.9 copy.787
  236.9 1.9 copy.781
  238.8 1.9 copy.774
  240.7 1.9 copy.768
  242.5 1.9 copy.760
  244.4 1.7 bitcast_reduce_fusion.2
  258.6 1.8 multiply_reduce_fusion.6
  260.4 1.7 multiply_reduce_fusion.5
  262.1 1.7 multiply_reduce_fusion.4
  267.0 1.7 multiply_reduce_fusion.7
  268.7 3.9 multiply_reduce_fusion.3
  274.5 7.7 %multiply_convert_fusion.3 = (bf16[2,4,128,640]{2,3,0,1:T(8,128)(2,1)}, bf16[2,4,128,640]{2,3,0,1:T(8,128)(2,1)}, bf16[2,4,128,640]{2,3,0,1:T(8,128)(2,1)}, bf16...) fusion(f32[4,640,2,128]{3,1,2,0:T(8,128)} %get-tuple-element.16, ...), kind=kLoop, calls=%fused_computation.61 | loop fusion | flops 20971520 | bytes 32145408 | tf_op jit(solution)/shard_map/convert_element_type | solution.py:160
  282.3 2.7 fusion.41
  284.9 2.2 copy.864
  287.1 2.7 fusion.42
  289.8 2.2 copy.865
  292.0 2.7 fusion.43
  294.7 2.2 copy.866
  296.8 2.7 fusion.44
  299.5 2.2 copy.867
  301.7 2.7 fusion.118
  304.3 2.2 copy.868
  306.5 2.6 fusion.114
  309.1 2.2 copy.869
  311.3 2.7 fusion.110
  314.0 2.1 copy.870
  316.1 2.7 fusion.106
  318.8 2.2 copy.871
  328.6 2.3 copy.845
  330.9 2.3 copy.846
  333.2 2.3 copy.847
  335.5 2.3 copy.844
  337.8 2.3 multiply_convert_fusion.9
  369.5 2.3 copy.842
  374.8 7.4 %all-to-all-start.2 = ((bf16[3,16,8,2048]{3,2,0,1:T(8,128)(2,1)}), bf16[3,16,8,2048]{3,2,0,1:T(8,128)(2,1)}, u32[]{:S(2)}, u32[]{:S(2)}) async-start(bf16[3,16,8,2048]{3,2,0,1:T(8,128)(2,1)} %copy.872), calls=%async_computation.2 | async-start | bytes 3145728 | tf_op jit(solution)/shard_map/all_to_all | solution.py:52
  394.2 2.6 copy-done.15
  397.0 29.2 %all-to-all-done.2 = bf16[3,16,8,2048]{3,2,0,1:T(8,128)(2,1)} async-done(((bf16[3,16,8,2048]{3,2,0,1:T(8,128)(2,1)}), bf16[3,16,8,2048]{3,2,0,1:T(8,128)(2,1)}, u32[]{:S(2)}, u32[]{:S(2)}) %all-to-all-start.2) | async-done | bytes 1572896 | tf_op jit(solution)/shard_map/all_to_all | solution.py:52
  426.2 2.6 slice_bitcast_fusion.7
  428.7 2.5 gather_fusion.3
  431.3 2.5 gather_fusion.5
  433.8 2.5 gather_fusion.4
  439.1 6.0 %all-to-all-start.3 = ((bf16[3,16,8,2048]{3,2,0,1:T(8,128)(2,1)}), bf16[3,16,8,2048]{3,2,0,1:T(8,128)(2,1)}, u32[]{:S(2)}, u32[]{:S(2)}) async-start(bf16[3,16,8,2048]{3,2,0,1:T(8,128)(2,1)} %copy.873), calls=%async_computation.3 | async-start | bytes 3145728 | tf_op jit(solution)/shard_map/all_to_all | solution.py:54
  445.2 2.5 fusion
  450.1 2.1 fusion.98
  454.6 5.8 %collective-permute-done.2 = bf16[128,2048]{1,0:T(8,128)(2,1)} collective-permute-done((bf16[128,2048]{1,0:T(8,128)(2,1)}, bf16[128,2048]{1,0:T(8,128)(2,1)}, u32[]{:S(2)}, u32[]{:S(2)}) %collective-permute-start.2) | collective-permute-done | bytes 524320 | tf_op jit(solution)/shard_map/ppermute | solution.py:24
  461.9 3.3 collective-permute-done.3
  466.5 81.9 %all-reduce.5.cloned.1.call-done = f32[256,2048]{1,0:T(8,128)} async-done(((f32[256,2048]{1,0:T(8,128)}), f32[256,2048]{1,0:T(8,128)}) %all-reduce.5.cloned.1.call-update) | async-done | bytes 2097168 | tf_op jit(solution)/shard_map/psum | solution.py:210
  548.4 1.6 fusion.92
  (405 shorter events, 119.2 us)
Async XLA Ops:
  7.2 6.6 %copy-start = (s32[3,2,16]{2,1,0:T(2,128)S(1)}, s32[3,2,16]{2,1,0:T(2,128)}, u32[]{:S(2)}) copy-start(s32[3,2,16]{2,1,0:T(2,128)} %param.22) | copy-start | bytes 1156
  7.2 12.4 %copy-start.84 = (bf16[256,1024]{1,0:T(8,128)(2,1)S(1)}, bf16[256,1024]{1,0:T(8,128)(2,1)}, u32[]{:S(2)}) copy-start(bf16[256,1024]{1,0:T(8,128)(2,1)} %param.18) | copy-start | bytes 1572868
  22.5 6.7 %copy-start.104 = (s32[3,2,16]{2,1,0:T(2,128)S(1)}, s32[3,2,16]{2,1,0:T(2,128)}, u32[]{:S(2)}) copy-start(s32[3,2,16]{2,1,0:T(2,128)} %param.21) | copy-start | bytes 1156
  22.5 42.2 %all-to-all-start = ((bf16[3,16,8,2048]{3,2,0,1:T(8,128)(2,1)}), bf16[3,16,8,2048]{3,2,0,1:T(8,128)(2,1)S(1)}, u32[]{:S(2)}, u32[]{:S(2)}) async-start(bf16[3,16,8,2048]{3,2,0,1:T(8,128)(2,1)} %pad_maximum_fusion.1), calls=%async_computation | async-start | bytes 3145728 | tf_op jit(solution)/shard_map/all_to_all | solution.py:52
  71.2 7.3 %copy-start.95 = (s32[256,128]{1,0:T(8,128)S(1)}, s32[256,128]{1,0:T(8,128)}, u32[]{:S(2)}) copy-start(s32[256,128]{1,0:T(8,128)} %param.20) | copy-start | bytes 393220
  71.2 51.0 %all-to-all-start.1 = ((bf16[3,16,8,2048]{3,2,0,1:T(8,128)(2,1)}), bf16[3,16,8,2048]{3,2,0,1:T(8,128)(2,1)}, u32[]{:S(2)}, u32[]{:S(2)}) async-start(bf16[3,16,8,2048]{3,2,0,1:T(8,128)(2,1)} %copy.750), calls=%async_computation.1 | async-start | bytes 3145728 | tf_op jit(solution)/shard_map/all_to_all | solution.py:54
  76.7 149.1 %all-reduce.7.cloned.1.call-start = ((), (), s32[]{:S(2)}) async-start(), calls=%async_computation.5 | async-start | bytes 2097152 | tf_op jit(solution)/shard_map/psum | solution.py:32
  76.8 15.5 %collective-permute-start = (bf16[128,2048]{1,0:T(8,128)(2,1)}, bf16[128,2048]{1,0:T(8,128)(2,1)}, u32[]{:S(2)}, u32[]{:S(2)}) collective-permute-start(bf16[128,2048]{1,0:T(8,128)(2,1)} %get-tuple-element.116), channel_id=1, source_target_pairs={{0,1},{1,2},{2,3},{3,4},{4,5},{5,6},{6,7},{7,8},{8,9},{9,10},{10,1... | collective-permute-start | bytes 1572872 | tf_op jit(solution)/shard_map/ppermute | solution.py:24
  78.3 17.3 %collective-permute-start.1 = (bf16[128,2048]{1,0:T(8,128)(2,1)}, bf16[128,2048]{1,0:T(8,128)(2,1)}, u32[]{:S(2)}, u32[]{:S(2)}) collective-permute-start(bf16[128,2048]{1,0:T(8,128)(2,1)} %get-tuple-element.122), channel_id=1, source_target_pairs={{1,0},{2,1},{3,2},{4,3},{5,4},{6,5},{7,6},{8,7},{9,8},{10,9},{11,1... | collective-permute-start | bytes 1572872 | tf_op jit(solution)/shard_map/ppermute | solution.py:25
  82.7 2.7 copy-start.86
  84.2 4.3 slice-start
  85.1 20.5 %copy-start.50 = (bf16[2,128,256]{1,2,0:T(8,128)(2,1)}, bf16[2,128,256]{1,2,0:T(8,128)(2,1)S(1)}, u32[]{:S(2)}) copy-start(bf16[2,128,256]{1,2,0:T(8,128)(2,1)S(1)} %copy.941) | copy-start | bytes 393220
  85.2 22.0 %copy-start.48 = (bf16[2,128,256]{1,2,0:T(8,128)(2,1)}, bf16[2,128,256]{1,2,0:T(8,128)(2,1)S(1)}, u32[]{:S(2)}) copy-start(bf16[2,128,256]{1,2,0:T(8,128)(2,1)S(1)} %copy.940) | copy-start | bytes 393220
  85.3 3.2 slice-start.1
  85.4 19.2 %copy-start.42 = (bf16[2,128,256]{1,2,0:T(8,128)(2,1)}, bf16[2,128,256]{1,2,0:T(8,128)(2,1)S(1)}, u32[]{:S(2)}) copy-start(bf16[2,128,256]{1,2,0:T(8,128)(2,1)S(1)} %copy.942) | copy-start | bytes 393220
  102.3 5.0 copy-start.26
  103.4 2.2 copy-start.28
  103.7 3.6 copy-start.22
  251.5 1.9 copy-start.67
  255.7 1.8 copy-start.69
  258.6 1.8 copy-start.36
  260.4 1.7 copy-start.30
  262.1 1.7 copy-start.46
  262.1 1.7 copy-start.62
  265.1 1.9 copy-start.32
  267.0 1.7 copy-start.20
  267.0 1.7 copy-start.73
  272.7 9.6 %copy-start.96 = (f32[2,4,128]{2,1,0:T(4,128)}, f32[2,4,128]{2,1,0:T(4,128)S(1)}, u32[]{:S(2)}) copy-start(f32[2,4,128]{2,1,0:T(4,128)S(1)} %copy_add_fusion) | copy-start | bytes 12292
  273.3 8.9 %copy-start.98 = (f32[2,4,128]{2,1,0:T(4,128)}, f32[2,4,128]{2,1,0:T(4,128)S(1)}, u32[]{:S(2)}) copy-start(f32[2,4,128]{2,1,0:T(4,128)S(1)} %copy_add_fusion.2) | copy-start | bytes 12292
  273.9 8.3 %copy-start.101 = (f32[2,4,128]{2,1,0:T(4,128)}, f32[2,4,128]{2,1,0:T(4,128)S(1)}, u32[]{:S(2)}) copy-start(f32[2,4,128]{2,1,0:T(4,128)S(1)} %copy_add_fusion.3) | copy-start | bytes 12292
  337.8 2.4 copy-start.19
  337.8 2.4 copy-start.102
  340.1 1.9 copy-start.18
  340.1 1.9 copy-start.99
  342.4 2.1 copy-start.13
  342.4 2.1 copy-start.72
  344.5 1.8 copy-start.29
  344.8 2.3 copy-start.12
  344.8 2.3 copy-start.68
  349.1 2.1 copy-start.27
  349.8 2.4 copy-start.10
  349.8 2.4 copy-start.65
  358.3 6.3 %copy-start.60 = (f32[2,4,384,64]{2,3,1,0:T(8,128)S(1)}, f32[2,4,384,64]{2,3,1,0:T(8,128)}, u32[]{:S(2)}) copy-start(f32[2,4,384,64]{2,3,1,0:T(8,128)} %convolution_multiply_fusion.6) | copy-start | bytes 2359300
  365.8 7.8 %copy-start.16 = (bf16[384,2048]{1,0:T(8,128)(2,1)S(1)}, bf16[384,2048]{1,0:T(8,128)(2,1)}, u32[]{:S(2)}) copy-start(bf16[384,2048]{1,0:T(8,128)(2,1)} %slice.504) | copy-start | bytes 4718596
  374.8 7.5 %copy-start.31 = (bf16[2,384,256]{1,2,0:T(8,128)(2,1)S(1)}, bf16[2,384,256]{1,2,0:T(8,128)(2,1)}, u32[]{:S(2)}) copy-start(bf16[2,384,256]{1,2,0:T(8,128)(2,1)} %copy.791) | copy-start | bytes 1179652
  374.8 7.5 %copy-start.83 = (f32[2,128,4,64]{1,3,2,0:T(8,128)S(1)}, f32[2,128,4,64]{1,3,2,0:T(8,128)}, u32[]{:S(2)}) copy-start(f32[2,128,4,64]{1,3,2,0:T(8,128)} %fusion.66) | copy-start | bytes 786436
  374.8 51.4 %all-to-all-start.2 = ((bf16[3,16,8,2048]{3,2,0,1:T(8,128)(2,1)}), bf16[3,16,8,2048]{3,2,0,1:T(8,128)(2,1)}, u32[]{:S(2)}, u32[]{:S(2)}) async-start(bf16[3,16,8,2048]{3,2,0,1:T(8,128)(2,1)} %copy.872), calls=%async_computation.2 | async-start | bytes 3145728 | tf_op jit(solution)/shard_map/all_to_all | solution.py:52
  382.2 166.2 %all-reduce.5.cloned.1.call-start = ((), (), s32[]{:S(2)}) async-start(), calls=%async_computation.4 | async-start | bytes 4194304 | tf_op jit(solution)/shard_map/psum | solution.py:210
  384.6 2.8 copy-start.7
  386.0 2.8 copy-start.23
  394.1 2.6 copy-start.15
  439.1 111.4 %all-to-all-start.3 = ((bf16[3,16,8,2048]{3,2,0,1:T(8,128)(2,1)}), bf16[3,16,8,2048]{3,2,0,1:T(8,128)(2,1)}, u32[]{:S(2)}, u32[]{:S(2)}) async-start(bf16[3,16,8,2048]{3,2,0,1:T(8,128)(2,1)} %copy.873), calls=%async_computation.3 | async-start | bytes 3145728 | tf_op jit(solution)/shard_map/all_to_all | solution.py:54
  447.7 4.7 copy-start.6
  447.7 4.5 copy-start.88
  447.7 4.5 copy-start.89
  447.8 4.5 copy-start.91
  447.8 4.5 copy-start.93
  447.8 4.5 copy-start.87
  447.8 4.5 copy-start.90
  447.8 4.5 copy-start.92
  447.8 4.5 copy-start.94
  448.7 11.7 %collective-permute-start.2 = (bf16[128,2048]{1,0:T(8,128)(2,1)}, bf16[128,2048]{1,0:T(8,128)(2,1)}, u32[]{:S(2)}, u32[]{:S(2)}) collective-permute-start(bf16[128,2048]{1,0:T(8,128)(2,1)} %slice.505), channel_id=1, source_target_pairs={{0,1},{1,2},{2,3},{3,4},{4,5},{5,6},{6,7},{7,8},{8,9},{9,10},{10,1... | collective-permute-start | bytes 1572872 | tf_op jit(solution)/shard_map/ppermute | solution.py:24
  452.2 13.0 %collective-permute-start.3 = (bf16[128,2048]{1,0:T(8,128)(2,1)}, bf16[128,2048]{1,0:T(8,128)(2,1)}, u32[]{:S(2)}, u32[]{:S(2)}) collective-permute-start(bf16[128,2048]{1,0:T(8,128)(2,1)} %fusion.98), channel_id=1, source_target_pairs={{1,0},{2,1},{3,2},{4,3},{5,4},{6,5},{7,6},{8,7},{9,8},{10,9},{11,1... | collective-permute-start | bytes 1572872 | tf_op jit(solution)/shard_map/ppermute | solution.py:25
  548.4 1.9 copy-start.82
  (53 other events, 65.2 us)
Sparse Core Ops, SparseCore 0:
  83.5 142.3 all-reduce.6
  390.1 158.2 all-reduce.4
where the time goes:
time: 572 us; the launch traced here: 563 us
  waiting for transfers between devices  274 us (48%)
  local copies, waits for them, and re-layouts  133 us (23%)
  matrix products  64.1 us (11%)
  other arithmetic  39.9 us (7%)
  starting transfers between devices  28.7 us (5%)
  between operations  23.1 us (4%)
    psum x1, waiting for transfers between devices, spread(): return lax.psum(jnp.where(mine, value, jnp.zeros_like(value)), axis)  101 us
    psum x1, waiting for transfers between devices, body(): global_sum = lax.psum(far_grads[:NGLOBAL * BLOCK], ('row', 'col'))  81.9 us
    all_to_all x2, waiting for transfers between devices, route_blocks(): lax.all_to_all(split_rows, 'col', split_axis=1, concat_axis=1, tiled=True)  64.7 us
    unnamed x249, local copies, waits for them, and re-layouts  35.2 us
    slice x19, local copies, waits for them, and re-layouts, split_heads(): part_cols = array[..., lower:upper]  22.8 us
    all_to_all x2, starting transfers between devices, route_blocks(): lax.all_to_all(split_rows, 'col', split_axis=1, concat_axis=1, tiled=True)  14.1 us
    all_to_all x2, waiting for transfers between devices, route_blocks(): lax.all_to_all(arranged, 'col', split_axis=1, concat_axis=1, tiled=True)  12.8 us
    all_to_all x2, starting transfers between devices, route_blocks(): lax.all_to_all(arranged, 'col', split_axis=1, concat_axis=1, tiled=True)  11.6 us
  transfers between devices with their start and end apart: 10, of which 9 were waited for; matrix products, arithmetic and copies ran while one was open for 11% of the time, Pallas kernels for 0%

commit v1 on v0

v1 whole, which is shorter than its diff:
```python
import functools

import jax
import jax.numpy as jnp
from jax import lax
from jax.experimental import pallas as pl
from jax.experimental.pallas import tpu as pltpu
from jax.sharding import PartitionSpec as P

HEADS = 16
HEAD_DIM = 64
BLOCK = 128
NGLOBAL = 2
NMATCH = 3
PAIR = 2 * HEAD_DIM
SLOTS = 3 + NGLOBAL + NMATCH
CHUNKS = 1

score_scale = 0.125
keep_scale = 1.0 / 0.9


def contract(a, b, dim_a, dim_b):
    return lax.dot_general(a, b, (((dim_a,), (dim_b,)), ((), ())), preferred_element_type=jnp.float32)


def attention_kernel(
    blocks, q_ref, g_ref, ko_ref, vo_ref, kp_ref, vp_ref, kn_ref, vn_ref, kg_ref, vg_ref, kr_ref, vr_ref, bits_ref,
    att_ref, qg_ref, own_ref, rims_ref, far_ref,
    keep_ref, kall_ref, vall_ref, qall_ref, gall_ref, s_ref, dp_ref, p_ref, ds_ref,
):
    near = blocks + 2
    own_rows = blocks * BLOCK

    @pl.when(pl.program_id(0) == 0)
    def _():
        shifts = lax.broadcasted_iota(jnp.int32, (BLOCK // 8, 8, BLOCK), 1)
        for j in range(blocks):
            for i in range(SLOTS):
                words = bits_ref[j, i * BLOCK // 8 : (i + 1) * BLOCK // 8, :]
                flags = jnp.right_shift(jnp.broadcast_to(words[:, None, :], shifts.shape), shifts) & 1
                keep_ref[j, i] = (flags.astype(jnp.float32) * keep_scale).reshape(BLOCK, BLOCK)
        p_ref[...] = jnp.zeros_like(p_ref)
        ds_ref[...] = jnp.zeros_like(ds_ref)

    for all_ref, parts in ((kall_ref, (kp_ref, ko_ref, kn_ref, kg_ref, kr_ref)), (vall_ref, (vp_ref, vo_ref, vn_ref, vg_ref, vr_ref))):
        row = 0
        for part in parts:
            all_ref[row : row + part.shape[0], :] = part[...]
            row += part.shape[0]
    first = lax.broadcasted_iota(jnp.int32, (BLOCK, PAIR), 1) < HEAD_DIM
    zero = jnp.zeros((BLOCK, PAIR), jnp.bfloat16)
    for j in range(blocks):
        rows = slice(j * BLOCK, (j + 1) * BLOCK)
        query = (q_ref[rows, :].astype(jnp.float32) * score_scale).astype(jnp.bfloat16)
        grad = g_ref[rows, :]
        base = 2 * j * BLOCK
        qall_ref[base : base + BLOCK, :] = jnp.where(first, query, zero)
        qall_ref[base + BLOCK : base + 2 * BLOCK, :] = jnp.where(first, zero, query)
        gall_ref[base : base + BLOCK, :] = jnp.where(first, grad, zero)
        gall_ref[base + BLOCK : base + 2 * BLOCK, :] = jnp.where(first, zero, grad)

    wide = 2 * BLOCK
    for j in range(blocks):
        cols = slice(j * wide, (j + 1) * wide)
        places = [j, j + 1, j + 2] + list(range(near, near + NGLOBAL + NMATCH))
        query = qall_ref[cols, :]
        grad = gall_ref[cols, :]
        top = None
        for i, b in enumerate(places):
            score = contract(kall_ref[b * BLOCK : (b + 1) * BLOCK, :], query, 1, 1)
            s_ref[i] = score
            part = jnp.max(score.reshape(BLOCK // 8, 8, wide), axis=0)
            top = part if top is None else jnp.maximum(top, part)
        top = jnp.max(top, axis=0, keepdims=True)
        total, mixed = None, None
        for i, b in enumerate(places):
            keep = keep_ref[j, i]
            keep = jnp.concatenate([keep, keep], axis=1)
            weight = jnp.exp(s_ref[i] - top)
            s_ref[i] = weight
            grad_p = contract(vall_ref[b * BLOCK : (b + 1) * BLOCK, :], grad, 1, 1) * keep
            dp_ref[i] = grad_p
            part = jnp.sum(weight.reshape(BLOCK // 8, 8, wide), axis=0)
            cross = jnp.sum((weight * grad_p).reshape(BLOCK // 8, 8, wide), axis=0)
            total = part if total is None else total + part
            mixed = cross if mixed is None else mixed + cross
        inverse = 1.0 / jnp.sum(total, axis=0, keepdims=True)
        delta = jnp.sum(mixed, axis=0, keepdims=True) * inverse
        for i, b in enumerate(places):
            keep = keep_ref[j, i]
            keep = jnp.concatenate([keep, keep], axis=1)
            probs = s_ref[i] * inverse
            p_ref[b * BLOCK : (b + 1) * BLOCK, cols] = (probs * keep).astype(jnp.bfloat16)
            ds_ref[b * BLOCK : (b + 1) * BLOCK, cols] = (probs * (dp_ref[i] - delta)).astype(jnp.bfloat16)

    out_t = contract(vall_ref[...], p_ref[...], 0, 0)
    qg_t = contract(kall_ref[...], ds_ref[...], 0, 0) * score_scale
    for j in range(blocks):
        rows = slice(j * BLOCK, (j + 1) * BLOCK)
        base = j * wide
        for result, ref in ((out_t, att_ref), (qg_t, qg_ref)):
            picked = jnp.concatenate(
                [result[:HEAD_DIM, base : base + BLOCK], result[HEAD_DIM:, base + BLOCK : base + wide]], axis=0
            )
            ref[rows, :] = picked.T.astype(jnp.bfloat16)
    for which, (left, right) in enumerate(((ds_ref, qall_ref), (p_ref, gall_ref))):
        grads = contract(left[...], right[...], 1, 0)
        own_ref[which] = grads[BLOCK : BLOCK + own_rows]
        rims_ref[which, :BLOCK] = grads[:BLOCK].astype(jnp.bfloat16)
        rims_ref[which, BLOCK:] = grads[BLOCK + own_rows : near * BLOCK].astype(jnp.bfloat16)
        far_ref[which] = grads[near * BLOCK :].astype(jnp.bfloat16)


def attention(queries, out_grad, key_rows, value_rows, before, after, shared, fetched, bits, chunk):
    tokens_here, width = queries.shape
    blocks = tokens_here // BLOCK
    pairs = width // PAIR // CHUNKS
    start = chunk * pairs
    part_width = width // CHUNKS
    far_rows = (NGLOBAL + NMATCH) * BLOCK
    all_rows = (blocks + 2) * BLOCK + far_rows

    def plain(rows):
        return pl.BlockSpec((rows, PAIR), lambda h: (0, start + h))

    def halves(rows):
        return [pl.BlockSpec((rows, PAIR), lambda h: (0, h)), pl.BlockSpec((rows, PAIR), lambda h: (0, pairs + h))]

    def out(rows, kind):
        return pl.BlockSpec((2, rows, PAIR), lambda h: (0, 0, h)), jax.ShapeDtypeStruct((2, rows, part_width), kind)

    flat = pl.BlockSpec((tokens_here, PAIR), lambda h: (0, h)), jax.ShapeDtypeStruct((tokens_here, part_width), jnp.bfloat16)
    outs = [flat, flat, out(tokens_here, jnp.float32), out(2 * BLOCK, jnp.bfloat16), out(far_rows, jnp.bfloat16)]
    pair_work = HEADS // CHUNKS * tokens_here * SLOTS * BLOCK
    return pl.pallas_call(
        functools.partial(attention_kernel, blocks),
        grid=(pairs,),
        in_specs=[plain(tokens_here)] * 4
        + halves(BLOCK) + halves(BLOCK) + halves(NGLOBAL * BLOCK) + halves(NMATCH * BLOCK)
        + [pl.BlockSpec(bits.shape, lambda h: (0, 0, 0))],
        out_specs=[spec for spec, _ in outs],
        out_shape=[shape for _, shape in outs],
        scratch_shapes=[
            pltpu.VMEM((blocks, SLOTS, BLOCK, BLOCK), jnp.float32),
            pltpu.VMEM((all_rows, PAIR), jnp.bfloat16),
            pltpu.VMEM((all_rows, PAIR), jnp.bfloat16),
            pltpu.VMEM((2 * tokens_here, PAIR), jnp.bfloat16),
            pltpu.VMEM((2 * tokens_here, PAIR), jnp.bfloat16),
            pltpu.VMEM((SLOTS, BLOCK, 2 * BLOCK), jnp.float32),
            pltpu.VMEM((SLOTS, BLOCK, 2 * BLOCK), jnp.float32),
            pltpu.VMEM((all_rows, 2 * tokens_here), jnp.bfloat16),
            pltpu.VMEM((all_rows, 2 * tokens_here), jnp.bfloat16),
        ],
        cost_estimate=pl.CostEstimate(
            flops=pair_work * HEAD_DIM * 2 * 7, bytes_accessed=16 * tokens_here * part_width, transcendentals=pair_work
        ),
        name="block_attention",
    )(queries, out_grad, key_rows, value_rows, before, before, after, after, shared, shared, fetched, fetched, bits)


def exchange(pieces):
    return lax.all_to_all(pieces, "col", split_axis=0, concat_axis=0, tiled=True)


def body(queries, key_rows, value_rows, out_grad, dropout_bits, partner, block_pick, global_blocks):
    tokens_here, width = queries.shape
    blocks = tokens_here // BLOCK
    bands, cols = lax.axis_size("row"), lax.axis_size("col")
    band, place = lax.axis_index("row"), lax.axis_index("col")
    rows = BLOCK // cols
    part = width // CHUNKS
    size = bands * cols
    up = [(i, (i + 1) % size) for i in range(size)]
    down = [(j, i) for i, j in up]
    ordering = lax.dynamic_index_in_dim(partner, band, 1, keepdims=False)
    picks = lax.dynamic_index_in_dim(block_pick, band, 1, keepdims=False)
    col_ids = jnp.arange(cols, dtype=jnp.int32)
    hits = ordering[:, :, None] == col_ids[None, None, :]
    inverse = jnp.sum(jnp.where(hits, col_ids[None, :, None], 0), axis=1)
    asked = jnp.sum(jnp.where(hits, picks[:, :, None], 0), axis=1)
    wanted_ids = (ordering * blocks + picks).T.reshape(-1)
    band_start = band * cols * blocks
    global_ids = jnp.clip(global_blocks - band_start, 0, cols * blocks - 1)
    bits = dropout_bits.reshape(blocks, BLOCK, -1).swapaxes(1, 2)
    attended, query_grad, key_grad, value_grad = [], [], [], []
    for chunk in range(CHUNKS):
        lower, upper = chunk * part, (chunk + 1) * part
        both = jnp.concatenate([key_rows[:, lower:upper], value_rows[:, lower:upper]], 1)
        spread = exchange(both.reshape(blocks, cols, rows, 2 * part).swapaxes(0, 1))
        strips = spread.reshape(cols * blocks, rows, 2 * part)
        global_strips = jnp.take(strips, global_ids, axis=0)
        gathered = lax.all_gather(global_strips, ("row", "col"), axis=0, tiled=False)
        gathered = gathered.reshape(bands, cols, NGLOBAL, rows, 2 * part)
        shared = jnp.concatenate(
            [
                lax.dynamic_index_in_dim(
                    gathered[:, :, g], global_blocks[g] // (cols * blocks), 0, keepdims=False
                ).reshape(BLOCK, 2 * part)
                for g in range(NGLOBAL)
            ],
            0,
        )
        sent = jnp.take(strips, wanted_ids, axis=0).reshape(cols, NMATCH, rows, 2 * part)
        fetched = exchange(sent).swapaxes(0, 1).reshape(NMATCH * BLOCK, 2 * part)
        before = lax.ppermute(both[tokens_here - BLOCK :], ("row", "col"), up)
        after = lax.ppermute(both[:BLOCK], ("row", "col"), down)
        att, qgrad, own, rims, far = attention(
            queries, out_grad, key_rows, value_rows, before, after, shared, fetched, bits, chunk
        )
        attended.append(att)
        query_grad.append(qgrad)
        from_next = lax.ppermute(rims[:, :BLOCK], ("row", "col"), down)
        from_last = lax.ppermute(rims[:, BLOCK:], ("row", "col"), up)
        slots = NGLOBAL + NMATCH
        pieces = far.reshape(2, slots, cols, rows, part).transpose(2, 1, 0, 3, 4)
        landed = exchange(pieces)
        band_sum = jnp.sum(landed[:, :NGLOBAL].astype(jnp.float32), axis=0)
        global_sum = band_sum
        for step in range(1, bands):
            ring = [(i, (i + step) % bands) for i in range(bands)]
            global_sum = global_sum + lax.ppermute(band_sum, "row", ring)
        block_ids = (band_start + jnp.arange(cols * blocks, dtype=jnp.int32)).reshape(cols, blocks)
        local_ids = jnp.arange(blocks, dtype=jnp.int32)
        returned = jnp.zeros((cols, blocks, 2, rows, part), jnp.float32)
        for matching in range(NMATCH):
            moved = jnp.take(landed[:, NGLOBAL + matching], inverse[matching], axis=0).astype(jnp.float32)
            mine = asked[matching][:, None] == local_ids[None, :]
            returned = returned + jnp.where(mine[:, :, None, None, None], moved[:, None], 0.0)
        for g in range(NGLOBAL):
            mine = block_ids == global_blocks[g]
            returned = returned + jnp.where(mine[:, :, None, None, None], global_sum[g][None, None], 0.0)
        home = exchange(returned.astype(jnp.bfloat16)).transpose(2, 1, 0, 3, 4).reshape(2, tokens_here, part)
        total = own + home.astype(jnp.float32)
        room = ((0, 0), (0, tokens_here - BLOCK), (0, 0))
        total = total + jnp.pad(from_last.astype(jnp.float32), room)
        total = total + jnp.pad(from_next.astype(jnp.float32), (room[0], room[1][::-1], room[2]))
        key_grad.append(total[0].astype(jnp.bfloat16))
        value_grad.append(total[1].astype(jnp.bfloat16))
    return tuple(jnp.concatenate(parts, 1) for parts in (attended, query_grad, key_grad, value_grad))


def solution(mesh):
    split = P(("row", "col"), None)
    return jax.shard_map(
        body,
        mesh=mesh,
        in_specs=(split,) * 5 + (P(),) * 3,
        out_specs=(split,) * 4,
        check_vma=False,
    )
```

time: 572 us -> 265 us (0.46); the launches traced: 563 us -> 264 us
  waiting for transfers between devices: 274 us -> 159 us
  local copies, waits for them, and re-layouts: 133 us -> 23.2 us
  matrix products: 64.1 us -> 0 us
  other arithmetic: 39.9 us -> 9.47 us
  Pallas kernels: 0 us -> 24.6 us
    psum x2 -> x0, waiting for transfers between devices: 183 us -> none  [the longest x1 101 us: spread(): return lax.psum(jnp.where(mine, value, jnp.zeros_like(value)), axis)]
    all_to_all x4, waiting for transfers between devices: 77.5 us -> 146 us  [exchange(): lax.all_to_all(pieces, 'col', split_axis=0, concat_axis=0, tiled=True)]
    dot_general x48 -> x0, matrix products: 64.1 us -> none  [the longest x4 10.7 us: body(): jnp.einsum('jgqk,jqgd->kgd', dscore_far, query_group, preferred_element_t...]
    unnamed x249 -> x21, local copies, waits for them, and re-layouts: 35.2 us -> 3.49 us
    slice x33 -> x4, local copies, waits for them, and re-layouts: 32.7 us -> 2.49 us  [the longest x1 1.68 us: body(): gathered[:, :, g]]
    reshape x16 -> x5, local copies, waits for them, and re-layouts: 32.6 us -> 5.61 us  [the longest x1 3.62 us: body(): pieces = far.reshape(2, slots, cols, rows, part).transpose(2, 1, 0, 3, 4)]
    pallas_call x0 -> x1, Pallas kernels: none -> 24.6 us  [attention(): pl.pallas_call(functools.partial(attention_kernel, blocks), grid=(pairs,)...]
    ppermute x4 -> x5, waiting for transfers between devices: 13.6 us -> 0.01 us  [the longest x1 0.01 us: body(): before = lax.ppermute(both[tokens_here - BLOCK:], ('row', 'col'), up)]
  transfers between devices with their start and end apart: 10 -> 10, of which waited for: 9 -> 5; matrix products, arithmetic and copies ran while one was open for 11% -> 7% of each run, Pallas kernels for 0% -> 0%
where the time goes in v1:
time: 265 us; the launch traced here: 264 us
  waiting for transfers between devices  159 us (60%)
  starting transfers between devices  28.6 us (11%)
  Pallas kernels  24.6 us (9%)
  local copies, waits for them, and re-layouts  23.2 us (9%)
  between operations  19.1 us (7%)
  other arithmetic  9.47 us (4%)
    all_to_all x4, waiting for transfers between devices, exchange(): lax.all_to_all(pieces, 'col', split_axis=0, concat_axis=0, tiled=True)  146 us
    all_to_all x4, starting transfers between devices, exchange(): lax.all_to_all(pieces, 'col', split_axis=0, concat_axis=0, tiled=True)  25 us
    pallas_call x1, Pallas kernels, attention(): pl.pallas_call(functools.partial(attention_kernel, blocks), grid=(pairs,)...  24.6 us
    all_gather x1, waiting for transfers between devices, body(): lax.all_gather(global_strips, ('row', 'col'), axis=0, tiled=False)  13 us
  transfers between devices with their start and end apart: 10, of which 5 were waited for; matrix products, arithmetic and copies ran while one was open for 7% of the time, Pallas kernels for 0%

profile of v1, /device:TPU:9, one launch (start us, length us, event | category | flops | bytes accessed | tf_op | source)
XLA Modules:
  0.0 263.9 jit_solution(8378470473770697904)
XLA Ops:
  7.2 0.0 copy-start
  7.2 1.1 constant_dynamic-update-slice_fusion.1
  8.3 1.1 constant_dynamic-update-slice_fusion
  9.4 0.0 copy-start.5
  9.4 0.0 copy-start.6
  9.4 1.0 copy.54
  10.4 6.5 %all-to-all-start = ((bf16[16,2,8,2048]{3,2,1,0:T(8,128)(2,1)}), bf16[16,2,8,2048]{3,2,1,0:T(8,128)(2,1)S(1)}, u32[]{:S(2)}, u32[]{:S(2)}) async-start(bf16[16,2,8,2048]{3,2,1,0:T(8,128)(2,1)} %bitcast.76), calls=%async_computation | async-start | bytes 2097152 | tf_op jit(solution)/shard_map/all_to_all | solution.py:163
  17.0 0.0 all-gather.2.cloned.1.call-start
  17.1 24.8 %all-to-all-done = bf16[16,2,8,2048]{3,2,1,0:T(8,128)(2,1)S(1)} async-done(((bf16[16,2,8,2048]{3,2,1,0:T(8,128)(2,1)}), bf16[16,2,8,2048]{3,2,1,0:T(8,128)(2,1)S(1)}, u32[]{:S(2)}, u32[]{:S(2)}) %all-to-all-start) | async-done | bytes 1048608 | tf_op jit(solution)/shard_map/all_to_all | solution.py:163
  41.9 0.5 gather_fusion
  42.5 0.7 bitcast_select_fusion
  43.2 0.0 all-gather.2.cloned.1.call-update
  43.2 0.1 copy.34
  43.3 0.1 reshape.201
  43.4 0.1 copy.33
  43.5 1.9 gather_fusion.1
  45.4 2.8 %broadcast_select_fusion = bf16[16,3,8,2048]{3,2,1,0:T(8,128)(2,1)} fusion(bf16[16,3,8,2048]{3,2,1,0:T(8,128)(2,1)} %bitcast.83, pred[16,3]{1,0:T(8,128)(4,1)S(1)} %copy.33), kind=kLoop, calls=%fused_computation.13 | loop fusion | flops 786432 | bytes 3145776 | tf_op jit(solution)/shard_map/jit(_take)/select_n | solution.py:204
  48.2 4.9 %all-to-all-start.1 = ((bf16[16,3,8,2048]{3,2,1,0:T(8,128)(2,1)}), bf16[16,3,8,2048]{3,2,1,0:T(8,128)(2,1)}, u32[]{:S(2)}, u32[]{:S(2)}) async-start(bf16[16,3,8,2048]{3,2,1,0:T(8,128)(2,1)} %broadcast_select_fusion), calls=%async_computation.1 | async-start | bytes 3145728 | tf_op jit(solution)/shard_map/all_to_all | solution.py:163
  53.1 0.1 fusion.8
  53.2 1.5 collective-permute-start
  54.7 0.0 collective-permute-start.1
  54.7 0.6 fusion.9
  60.1 0.7 copy.36
  60.8 37.1 %all-to-all-done.1 = bf16[16,3,8,2048]{3,2,1,0:T(8,128)(2,1)} async-done(((bf16[16,3,8,2048]{3,2,1,0:T(8,128)(2,1)}), bf16[16,3,8,2048]{3,2,1,0:T(8,128)(2,1)}, u32[]{:S(2)}, u32[]{:S(2)}) %all-to-all-start.1) | async-done | bytes 1572896 | tf_op jit(solution)/shard_map/all_to_all | solution.py:163
  97.9 2.7 %copy.35 = bf16[3,16,8,2048]{3,2,1,0:T(8,128)(2,1)} copy(bf16[3,16,8,2048]{3,2,0,1:T(8,128)(2,1)} %bitcast.12) | data formatting | bytes 3145728 | tf_op jit(solution)/shard_map/transpose | solution.py:205
  100.6 13.0 %all-gather.2.cloned.1.call-done = bf16[32,2,8,2048]{3,2,1,0:T(8,128)(2,1)} async-done(((bf16[1,2,8,2048]{3,2,1,0:T(8,128)(2,1)}), bf16[32,2,8,2048]{3,2,1,0:T(8,128)(2,1)}) %all-gather.2.cloned.1.call-update) | async-done | bytes 2097168 | tf_op jit(solution)/shard_map/all_gather | solution.py:193
  113.6 1.7 fusion.6
  115.3 0.1 dynamic-slice_bitcast_fusion
  115.4 1.1 pad_maximum_fusion.kg_ref.vg_ref
  116.6 0.0 collective-permute-done.kp_ref.vp_ref
  116.6 0.0 collective-permute-done.1.kn_ref.vn_ref
  116.6 0.0 copy-start.8
  116.6 0.8 copy-done.7
  117.4 0.2 copy-done.8
  117.5 24.6 %block_attention.1 = (bf16[256,1024]{1,0:T(8,128)(2,1)}, bf16[256,1024]{1,0:T(8,128)(2,1)}, f32[2,256,1024]{2,1,0:T(8,128)}, bf16[2,256,1024]{2,1,0:T(8,128)(2,1)}, bf16[2,640,1024]{2,1,0:T(8,128)(2,1)}) custom-call(bf16[256,1024]{1,0:T(8,128)(2,1)} %q_ref.1, bf16[256,1024]{1,0:T(8,128)(2,1)} %g_ref.1, bf16[256,1024]{1,0:T(8,128)(2,1)} %ko_ref.1, ...), custom_call_target="tpu_custom_call" | custom-call | flops 3758096384 | bytes 4194304 | tf_op jit(solution)/shard_map/block_attention/pallas_call | solution.py:136
  142.1 3.6 %copy.53 = bf16[2,5,16,8,1024]{4,3,1,0,2:T(8,128)(2,1)} copy(bf16[2,5,16,8,1024]{4,3,2,1,0:T(8,128)(2,1)} %bitcast.84) | data formatting | bytes 5242880 | tf_op jit(solution)/shard_map/reshape | solution.py:216
  145.7 5.7 %all-to-all-start.2 = ((bf16[16,5,2,8,1024]{4,3,1,2,0:T(8,128)(2,1)}), bf16[16,5,2,8,1024]{4,3,1,2,0:T(8,128)(2,1)S(1)}, u32[]{:S(2)}, u32[]{:S(2)}) async-start(bf16[16,5,2,8,1024]{4,3,1,2,0:T(8,128)(2,1)} %bitcast.79), calls=%async_computation.2 | async-start | bytes 5242880 | tf_op jit(solution)/shard_map/all_to_all | solution.py:163
  151.4 1.2 fusion.3
  152.6 0.1 select_reduce_fusion.1
  152.8 0.1 iota_compare_fusion.3
  152.9 0.1 iota_compare_fusion.1
  152.9 55.1 %all-to-all-done.2 = bf16[16,5,2,8,1024]{4,3,1,2,0:T(8,128)(2,1)S(1)} async-done(((bf16[16,5,2,8,1024]{4,3,1,2,0:T(8,128)(2,1)}), bf16[16,5,2,8,1024]{4,3,1,2,0:T(8,128)(2,1)S(1)}, u32[]{:S(2)}, u32[]{:S(2)}) %all-to-all-start.2) | async-done | bytes 2621472 | tf_op jit(solution)/shard_map/all_to_all | solution.py:163
  208.0 0.2 convert_reduce_fusion
  208.2 0.5 collective-permute-start.2
  208.7 1.1 slice_bitcast_fusion.4
  209.8 1.7 gather_fusion.4
  211.5 0.1 select_convert_fusion
  211.7 0.6 gather_fusion.3
  212.3 0.1 select_convert_fusion.1
  212.4 0.6 gather_fusion.2
  213.0 0.1 select_convert_fusion.2
  213.2 0.0 collective-permute-done.2
  213.2 1.9 add_convert_fusion
  215.1 7.9 %all-to-all-start.3 = ((bf16[16,2,2,8,1024]{4,3,1,2,0:T(8,128)(2,1)}), bf16[16,2,2,8,1024]{4,3,1,2,0:T(8,128)(2,1)S(1)}, u32[]{:S(2)}, u32[]{:S(2)}) async-start(bf16[16,2,2,8,1024]{4,3,1,2,0:T(8,128)(2,1)} %add_convert_fusion), calls=%async_computation.3 | async-start | bytes 2097152 | tf_op jit(solution)/shard_map/all_to_all | solution.py:163
  223.0 0.1 fusion.7
  223.0 1.5 collective-permute-start.3
  224.6 0.0 collective-permute-start.4
  224.6 28.9 %all-to-all-done.3 = bf16[16,2,2,8,1024]{4,3,1,2,0:T(8,128)(2,1)S(1)} async-done(((bf16[16,2,2,8,1024]{4,3,1,2,0:T(8,128)(2,1)}), bf16[16,2,2,8,1024]{4,3,1,2,0:T(8,128)(2,1)S(1)}, u32[]{:S(2)}, u32[]{:S(2)}) %all-to-all-start.3) | async-done | bytes 1048608 | tf_op jit(solution)/shard_map/all_to_all | solution.py:163
  253.5 0.2 convert_bitcast_fusion
  253.8 0.1 copy.39
  253.9 0.0 collective-permute-done.3
  253.9 1.4 copy-done.1
  255.3 0.6 fusion.2
  256.0 1.0 slice_bitcast_fusion
  (27 shorter events, 0.1 us)
Async XLA Ops:
  7.2 9.9 %copy-start = (s32[3,2,16]{2,1,0:T(2,128)S(1)}, s32[3,2,16]{2,1,0:T(2,128)}, u32[]{:S(2)}) copy-start(s32[3,2,16]{2,1,0:T(2,128)} %param.16) | copy-start | bytes 1156
  9.4 7.7 %copy-start.5 = (s32[2]{0:T(128)S(1)}, s32[2]{0:T(128)}, u32[]{:S(2)}) copy-start(s32[2]{0:T(128)} %param.17) | copy-start | bytes 28
  9.4 33.8 %copy-start.6 = (s32[3,2,16]{2,1,0:T(2,128)S(1)}, s32[3,2,16]{2,1,0:T(2,128)}, u32[]{:S(2)}) copy-start(s32[3,2,16]{2,1,0:T(2,128)} %param.15) | copy-start | bytes 1156
  10.4 31.5 %all-to-all-start = ((bf16[16,2,8,2048]{3,2,1,0:T(8,128)(2,1)}), bf16[16,2,8,2048]{3,2,1,0:T(8,128)(2,1)S(1)}, u32[]{:S(2)}, u32[]{:S(2)}) async-start(bf16[16,2,8,2048]{3,2,1,0:T(8,128)(2,1)} %bitcast.76), calls=%async_computation | async-start | bytes 2097152 | tf_op jit(solution)/shard_map/all_to_all | solution.py:163
  17.0 96.7 %all-gather.2.cloned.1.call-start = ((), (), s32[]{:S(2)}) async-start(), calls=%async_computation.4 | async-start | bytes 2162688 | tf_op jit(solution)/shard_map/all_gather | solution.py:193
  48.2 11.9 %copy-start.4 = (s32[256,128]{1,0:T(8,128)S(1)}, s32[256,128]{1,0:T(8,128)}, u32[]{:S(2)}) copy-start(s32[256,128]{1,0:T(8,128)} %param.14) | copy-start | bytes 393220
  48.2 49.8 %all-to-all-start.1 = ((bf16[16,3,8,2048]{3,2,1,0:T(8,128)(2,1)}), bf16[16,3,8,2048]{3,2,1,0:T(8,128)(2,1)}, u32[]{:S(2)}, u32[]{:S(2)}) async-start(bf16[16,3,8,2048]{3,2,1,0:T(8,128)(2,1)} %broadcast_select_fusion), calls=%async_computation.1 | async-start | bytes 3145728 | tf_op jit(solution)/shard_map/all_to_all | solution.py:163
  53.2 63.4 %collective-permute-start = (bf16[128,2048]{1,0:T(8,128)(2,1)S(1)}, bf16[128,2048]{1,0:T(8,128)(2,1)S(1)}, u32[]{:S(2)}, u32[]{:S(2)}) collective-permute-start(bf16[128,2048]{1,0:T(8,128)(2,1)S(1)} %get-tuple-element.37), channel_id=1, source_target_pairs={{0,1},{1,2},{2,3},{3,4},{4,5},{5,6},{6,7},{7,8},{8,9},{9,10},{10,1... | collective-permute-start | bytes 1572872 | tf_op jit(solution)/shard_map/ppermute | solution.py:206
  54.7 61.9 %collective-permute-start.1 = (bf16[128,2048]{1,0:T(8,128)(2,1)S(1)}, bf16[128,2048]{1,0:T(8,128)(2,1)S(1)}, u32[]{:S(2)}, u32[]{:S(2)}) collective-permute-start(bf16[128,2048]{1,0:T(8,128)(2,1)S(1)} %get-tuple-element.36), channel_id=1, source_target_pairs={{1,0},{2,1},{3,2},{4,3},{5,4},{6,5},{7,6},{8,7},{9,8},{10,9},{11,1... | collective-permute-start | bytes 1572872 | tf_op jit(solution)/shard_map/ppermute | solution.py:207
  116.6 0.8 copy-start.7
  116.6 1.0 copy-start.8
  145.7 62.3 %all-to-all-start.2 = ((bf16[16,5,2,8,1024]{4,3,1,2,0:T(8,128)(2,1)}), bf16[16,5,2,8,1024]{4,3,1,2,0:T(8,128)(2,1)S(1)}, u32[]{:S(2)}, u32[]{:S(2)}) async-start(bf16[16,5,2,8,1024]{4,3,1,2,0:T(8,128)(2,1)} %bitcast.79), calls=%async_computation.2 | async-start | bytes 5242880 | tf_op jit(solution)/shard_map/all_to_all | solution.py:163
  208.2 4.9 %collective-permute-start.2 = (f32[2,2,8,1024]{3,2,0,1:T(8,128)S(1)}, f32[2,2,8,1024]{3,2,0,1:T(8,128)S(1)}, u32[]{:S(2)}, u32[]{:S(2)}) collective-permute-start(f32[2,2,8,1024]{3,2,0,1:T(8,128)S(1)} %convert_reduce_fusion), channel_id=1, source_target_pairs={{0,16},{16,0},{1,17},{17,1},{2,18},{18,2},{3,19},{19,3},{4,20},{20... | collective-permute-start | bytes 393224 | tf_op jit(solution)/shard_map/ppermute | solution.py:222
  209.8 1.8 copy-start.2
  215.1 7.9 %copy-start.3 = (bf16[2,256,1024]{2,1,0:T(8,128)(2,1)S(1)}, bf16[2,256,1024]{2,1,0:T(8,128)(2,1)}, u32[]{:S(2)}) copy-start(bf16[2,256,1024]{2,1,0:T(8,128)(2,1)} %get-tuple-element.14) | copy-start | bytes 3145732
  215.1 38.4 %all-to-all-start.3 = ((bf16[16,2,2,8,1024]{4,3,1,2,0:T(8,128)(2,1)}), bf16[16,2,2,8,1024]{4,3,1,2,0:T(8,128)(2,1)S(1)}, u32[]{:S(2)}, u32[]{:S(2)}) async-start(bf16[16,2,2,8,1024]{4,3,1,2,0:T(8,128)(2,1)} %add_convert_fusion), calls=%async_computation.3 | async-start | bytes 2097152 | tf_op jit(solution)/shard_map/all_to_all | solution.py:163
  223.0 30.9 %collective-permute-start.3 = (bf16[2,128,1024]{2,1,0:T(8,128)(2,1)S(1)}, bf16[2,128,1024]{2,1,0:T(8,128)(2,1)S(1)}, u32[]{:S(2)}, u32[]{:S(2)}) collective-permute-start(bf16[2,128,1024]{2,1,0:T(8,128)(2,1)S(1)} %get-tuple-element.34), channel_id=1, source_target_pairs={{0,1},{1,2},{2,3},{3,4},{4,5},{5,6},{6,7},{7,8},{8,9},{9,10},{10,1... | collective-permute-start | bytes 1572872 | tf_op jit(solution)/shard_map/ppermute | solution.py:214
  224.6 29.4 %collective-permute-start.4 = (bf16[2,128,1024]{2,1,0:T(8,128)(2,1)S(1)}, bf16[2,128,1024]{2,1,0:T(8,128)(2,1)S(1)}, u32[]{:S(2)}, u32[]{:S(2)}) collective-permute-start(bf16[2,128,1024]{2,1,0:T(8,128)(2,1)S(1)} %get-tuple-element.35), channel_id=1, source_target_pairs={{1,0},{2,1},{3,2},{4,3},{5,4},{6,5},{7,6},{8,7},{9,8},{10,9},{11,1... | collective-permute-start | bytes 1572872 | tf_op jit(solution)/shard_map/ppermute | solution.py:213
  253.8 1.6 copy-start.1
Sparse Core Ops, SparseCore 0:
  43.3 70.2 all-gather.1

commit v2 on v1

--- a/solution.py
+++ b/solution.py
@@ -159,6 +159,101 @@
     )(queries, out_grad, key_rows, value_rows, before, before, after, after, shared, shared, fetched, fetched, bits)
 
 
+def partner_of(me, bit):
+    flag = (me // 2**bit) % 2
+    return flag, me + 2**bit - 2 * 2**bit * flag
+
+
+def greet(me, levels):
+    barrier = pltpu.get_barrier_semaphore()
+    for bit in range(levels):
+        pl.semaphore_signal(barrier, inc=1, device_id={"col": partner_of(me, bit)[1]})
+    pl.semaphore_wait(barrier, levels)
+
+
+def gather_kernel(levels, strip_ref, all_ref, send_sem, recv_sem):
+    me = lax.axis_index("col")
+    greet(me, levels)
+    flags = [partner_of(me, levels - 1 - d)[0] for d in range(levels)]
+    pick = pl.ds
+    here = tuple(pick(flag, 1) for flag in flags)
+    all_ref[here] = strip_ref[...].reshape((1,) * levels + strip_ref.shape)
+    for dim in range(levels):
+        region = (slice(None),) * dim + here[dim:]
+        copy = pltpu.make_async_remote_copy(
+            src_ref=all_ref.at[region],
+            dst_ref=all_ref.at[region],
+            send_sem=send_sem.at[dim],
+            recv_sem=recv_sem.at[dim],
+            device_id={"col": partner_of(me, levels - 1 - dim)[1]},
+        )
+        copy.start()
+        copy.wait()
+
+
+def gather_strips(strip, cols):
+    levels = cols.bit_length() - 1
+    vmem = pl.BlockSpec(memory_space=pltpu.VMEM)
+    out = pl.pallas_call(
+        functools.partial(gather_kernel, levels),
+        out_shape=jax.ShapeDtypeStruct((2,) * levels + strip.shape, strip.dtype),
+        in_specs=[vmem],
+        out_specs=vmem,
+        scratch_shapes=[pltpu.SemaphoreType.DMA((levels,)), pltpu.SemaphoreType.DMA((levels,))],
+        compiler_params=pltpu.CompilerParams(collective_id=1, has_side_effects=True),
+        cost_estimate=pl.CostEstimate(flops=2 * 10**10, bytes_accessed=3 * cols * strip.size, transcendentals=0),
+        name="gather_strips",
+    )(strip)
+    return out.reshape((cols,) + strip.shape)
+
+
+def reduce_kernel(levels, parts_ref, sum_ref, *scratch):
+    landing, sums, (send_sem, recv_sem) = scratch[:levels], scratch[levels : 2 * levels - 1], scratch[2 * levels - 1 :]
+    me = lax.axis_index("col")
+    greet(me, levels)
+    source = parts_ref
+    for bit in range(levels):
+        dim = levels - 1 - bit
+        flag, partner = partner_of(me, bit)
+        lead = (slice(None),) * dim
+        tail = (slice(None),) * (bit + 2)
+        copy = pltpu.make_async_remote_copy(
+            src_ref=source.at[lead + (pl.ds(1 - flag, 1),) + tail],
+            dst_ref=landing[bit],
+            send_sem=send_sem.at[bit],
+            recv_sem=recv_sem.at[bit],
+            device_id={"col": partner},
+        )
+        copy.start()
+        copy.wait()
+        mine = source[lead + (pl.ds(flag, 1),) + tail]
+        total = mine.astype(jnp.float32) + landing[bit][...].astype(jnp.float32)
+        if bit < levels - 1:
+            source = sums[bit]
+            source[...] = total
+        else:
+            sum_ref[...] = total.reshape(sum_ref.shape)
+
+
+def reduce_strips(parts):
+    cols, rows, width = parts.shape
+    levels = cols.bit_length() - 1
+    vmem = pl.BlockSpec(memory_space=pltpu.VMEM)
+    shapes = [(2,) * (levels - 1 - bit) + (1,) * (bit + 1) + (rows, width) for bit in range(levels)]
+    return pl.pallas_call(
+        functools.partial(reduce_kernel, levels),
+        out_shape=jax.ShapeDtypeStruct((rows, width), jnp.float32),
+        in_specs=[vmem],
+        out_specs=vmem,
+        scratch_shapes=[pltpu.VMEM(shape, jnp.float32 if bit else parts.dtype) for bit, shape in enumerate(shapes)]
+        + [pltpu.VMEM(shape, jnp.float32) for shape in shapes[:-1]]
+        + [pltpu.SemaphoreType.DMA((levels,)), pltpu.SemaphoreType.DMA((levels,))],
+        compiler_params=pltpu.CompilerParams(collective_id=2, has_side_effects=True),
+        cost_estimate=pl.CostEstimate(flops=2 * 10**10, bytes_accessed=3 * parts.size, transcendentals=0),
+        name="reduce_strips",
+    )(parts.reshape((2,) * levels + (rows, width)))
+
+
 def exchange(pieces):
     return lax.all_to_all(pieces, "col", split_axis=0, concat_axis=0, tiled=True)
 
@@ -190,17 +285,14 @@
         spread = exchange(both.reshape(blocks, cols, rows, 2 * part).swapaxes(0, 1))
         strips = spread.reshape(cols * blocks, rows, 2 * part)
         global_strips = jnp.take(strips, global_ids, axis=0)
-        gathered = lax.all_gather(global_strips, ("row", "col"), axis=0, tiled=False)
-        gathered = gathered.reshape(bands, cols, NGLOBAL, rows, 2 * part)
-        shared = jnp.concatenate(
-            [
-                lax.dynamic_index_in_dim(
-                    gathered[:, :, g], global_blocks[g] // (cols * blocks), 0, keepdims=False
-                ).reshape(BLOCK, 2 * part)
-                for g in range(NGLOBAL)
-            ],
-            0,
-        )
+        owners = global_blocks // (cols * blocks)
+        chosen = global_strips
+        for step in range(1, bands):
+            ring = [(i, (i + step) % bands) for i in range(bands)]
+            other = lax.ppermute(global_strips, "row", ring)
+            chosen = jnp.where((owners == (band - step) % bands)[:, None, None], other, chosen)
+        shared = gather_strips(chosen.reshape(NGLOBAL * rows, 2 * part), cols)
+        shared = shared.reshape(cols, NGLOBAL, rows, 2 * part).swapaxes(0, 1).reshape(NGLOBAL * BLOCK, 2 * part)
         sent = jnp.take(strips, wanted_ids, axis=0).reshape(cols, NMATCH, rows, 2 * part)
         fetched = exchange(sent).swapaxes(0, 1).reshape(NMATCH * BLOCK, 2 * part)
         before = lax.ppermute(both[tokens_here - BLOCK :], ("row", "col"), up)
@@ -214,8 +306,9 @@
         from_last = lax.ppermute(rims[:, BLOCK:], ("row", "col"), up)
         slots = NGLOBAL + NMATCH
         pieces = far.reshape(2, slots, cols, rows, part).transpose(2, 1, 0, 3, 4)
-        landed = exchange(pieces)
-        band_sum = jnp.sum(landed[:, :NGLOBAL].astype(jnp.float32), axis=0)
+        landed = exchange(pieces[:, NGLOBAL:])
+        strips_sum = reduce_strips(pieces[:, :NGLOBAL].reshape(cols, NGLOBAL * 2 * rows, part))
+        band_sum = strips_sum.reshape(NGLOBAL, 2, rows, part)
         global_sum = band_sum
         for step in range(1, bands):
             ring = [(i, (i + step) % bands) for i in range(bands)]
@@ -224,7 +317,7 @@
         local_ids = jnp.arange(blocks, dtype=jnp.int32)
         returned = jnp.zeros((cols, blocks, 2, rows, part), jnp.float32)
         for matching in range(NMATCH):
-            moved = jnp.take(landed[:, NGLOBAL + matching], inverse[matching], axis=0).astype(jnp.float32)
+            moved = jnp.take(landed[:, matching], inverse[matching], axis=0).astype(jnp.float32)
             mine = asked[matching][:, None] == local_ids[None, :]
             returned = returned + jnp.where(mine[:, :, None, None, None], moved[:, None], 0.0)
         for g in range(NGLOBAL):

time: 265 us -> 237 us (0.89)
  waiting for transfers between devices: 159 us -> 58.6 us
  Pallas kernels: 24.6 us -> 115 us
  between operations: 19.1 us -> 0.93 us
  starting transfers between devices: 28.6 us -> 32.2 us
    all_to_all x4, waiting for transfers between devices: 146 us -> 55 us  [exchange(): lax.all_to_all(pieces, 'col', split_axis=0, concat_axis=0, tiled=True)]
    pallas_call x0 -> x2, Pallas kernels: none -> 90.5 us  [the longest x1 48.8 us: gather_strips(): pl.pallas_call(functools.partial(gather_kernel, levels), out_shape=jax.Sh...]
    all_gather x1 -> x0, waiting for transfers between devices: 13 us -> none  [body(): lax.all_gather(global_strips, ('row', 'col'), axis=0, tiled=False)]
  transfers between devices with their start and end apart: 10 -> 10, of which waited for: 5 -> 4; matrix products, arithmetic and copies ran while one was open for 7% -> 6% of each run, Pallas kernels for 0% -> 38%
where the time goes in v2:
time: 237 us; the launch traced here: 236 us
  Pallas kernels  115 us (49%)
  waiting for transfers between devices  58.6 us (25%)
  starting transfers between devices  32.2 us (14%)
  local copies, waits for them, and re-layouts  21.1 us (9%)
  other arithmetic  7.84 us (3%)
    all_to_all x4, waiting for transfers between devices, exchange(): lax.all_to_all(pieces, 'col', split_axis=0, concat_axis=0, tiled=True)  55 us
    pallas_call x1, Pallas kernels, gather_strips(): pl.pallas_call(functools.partial(gather_kernel, levels), out_shape=jax.Sh...  48.8 us
    pallas_call x1, Pallas kernels, reduce_strips(): pl.pallas_call(functools.partial(reduce_kernel, levels), out_shape=jax.Sh...  41.7 us
    all_to_all x4, starting transfers between devices, exchange(): lax.all_to_all(pieces, 'col', split_axis=0, concat_axis=0, tiled=True)  26.3 us
    pallas_call x1, Pallas kernels, attention(): pl.pallas_call(functools.partial(attention_kernel, blocks), grid=(pairs,)...  24.5 us
  transfers between devices with their start and end apart: 10, of which 4 were waited for; matrix products, arithmetic and copies ran while one was open for 6% of the time, Pallas kernels for 38%

profile of v2, /device:TPU:9, one launch (start us, length us, event | category | flops | bytes accessed | tf_op | source)
XLA Modules:
  0.0 235.8 jit_solution(12819131476270959268)
XLA Ops:
  0.6 0.0 copy-start
  0.6 1.1 constant_dynamic-update-slice_fusion.1
  1.7 1.1 constant_dynamic-update-slice_fusion
  2.8 1.1 copy.57
  3.9 6.7 %all-to-all-start = ((bf16[16,2,8,2048]{3,2,1,0:T(8,128)(2,1)}), bf16[16,2,8,2048]{3,2,1,0:T(8,128)(2,1)S(1)}, u32[]{:S(2)}, u32[]{:S(2)}) async-start(bf16[16,2,8,2048]{3,2,1,0:T(8,128)(2,1)} %bitcast.77), calls=%async_computation | async-start | bytes 2097152 | tf_op jit(solution)/shard_map/all_to_all | solution.py:258
  10.6 0.9 fusion.8
  11.5 1.5 collective-permute-start
  12.9 0.0 collective-permute-start.1
  13.0 0.1 copy.39
  13.1 0.1 reshape.188
  13.2 0.1 copy.38
  13.3 0.0 copy-done.3
  13.3 0.8 copy.41
  14.0 0.0 copy-done.4
  14.1 0.6 fusion.9
  14.7 0.1 select_reduce_fusion.1
  14.8 26.3 %all-to-all-done = bf16[16,2,8,2048]{3,2,1,0:T(8,128)(2,1)S(1)} async-done(((bf16[16,2,8,2048]{3,2,1,0:T(8,128)(2,1)}), bf16[16,2,8,2048]{3,2,1,0:T(8,128)(2,1)S(1)}, u32[]{:S(2)}, u32[]{:S(2)}) %all-to-all-start) | async-done | bytes 1048608 | tf_op jit(solution)/shard_map/all_to_all | solution.py:258
  41.1 0.7 gather_fusion.1
  41.8 1.4 broadcast_select_fusion
  43.2 4.8 %all-to-all-start.1 = ((bf16[16,3,8,2048]{3,2,1,0:T(8,128)(2,1)}), bf16[16,3,8,2048]{3,2,1,0:T(8,128)(2,1)S(1)}, u32[]{:S(2)}, u32[]{:S(2)}) async-start(bf16[16,3,8,2048]{3,2,1,0:T(8,128)(2,1)} %broadcast_select_fusion), calls=%async_computation.1 | async-start | bytes 3145728 | tf_op jit(solution)/shard_map/all_to_all | solution.py:258
  48.0 0.6 gather_fusion
  48.5 0.1 broadcast_select_fusion.1
  48.6 1.2 collective-permute-start.2
  49.9 2.2 collective-permute-done.2
  52.0 0.7 select_bitcast_fusion.strip_ref
  52.7 48.8 %gather_strips.1 = bf16[2,2,2,2,16,2048]{5,4,3,2,1,0:T(8,128)(2,1)} custom-call(bf16[16,2048]{1,0:T(8,128)(2,1)} %select_bitcast_fusion.strip_ref), custom_call_target="tpu_custom_call" | custom-call | flops 20000000000 | bytes 1572864 | tf_op jit(solution)/shard_map/gather_strips/pallas_call | solution.py:197
  101.6 2.4 %copy.37 = bf16[16,2,8,2048]{3,2,0,1:T(8,128)(2,1)} copy(bf16[16,2,8,2048]{3,2,1,0:T(8,128)(2,1)} %bitcast.92) | data formatting | bytes 2097152 | tf_op jit(solution)/shard_map/reshape;reshape | solution.py:295
  104.0 0.0 all-to-all-done.1
  104.0 1.3 copy.40
  105.3 0.0 collective-permute-done.kp_ref.vp_ref
  105.3 0.0 collective-permute-done.1.kn_ref.vn_ref
  105.3 24.5 %block_attention.1 = (bf16[256,1024]{1,0:T(8,128)(2,1)}, bf16[256,1024]{1,0:T(8,128)(2,1)}, f32[2,256,1024]{2,1,0:T(8,128)}, bf16[2,256,1024]{2,1,0:T(8,128)(2,1)}, bf16[2,640,1024]{2,1,0:T(8,128)(2,1)}) custom-call(bf16[256,1024]{1,0:T(8,128)(2,1)} %q_ref.1, bf16[256,1024]{1,0:T(8,128)(2,1)} %g_ref.1, bf16[256,1024]{1,0:T(8,128)(2,1)} %ko_ref.1, ...), custom_call_target="tpu_custom_call" | custom-call | flops 3758096384 | bytes 4194304 | tf_op jit(solution)/shard_map/block_attention/pallas_call | solution.py:136
  129.9 2.1 copy.56
  131.9 1.3 slice.98
  133.3 4.4 %all-to-all-start.2 = ((bf16[16,3,2,8,1024]{4,3,2,1,0:T(8,128)(2,1)}), bf16[16,3,2,8,1024]{4,3,2,1,0:T(8,128)(2,1)}, u32[]{:S(2)}, u32[]{:S(2)}) async-start(bf16[16,3,2,8,1024]{4,3,2,1,0:T(8,128)(2,1)} %slice.98), calls=%async_computation.2 | async-start | bytes 3145728 | tf_op jit(solution)/shard_map/all_to_all | solution.py:258
  137.7 0.1 iota_compare_fusion.3
  137.8 0.1 iota_compare_fusion.1
  137.9 1.1 slice.102
  139.0 41.7 %reduce_strips.1 = f32[32,1024]{1,0:T(8,128)} custom-call(bf16[2,2,2,2,32,1024]{5,4,3,2,1,0:T(8,128)(2,1)} %bitcast.93), custom_call_target="tpu_custom_call" | custom-call | flops 20000000000 | bytes 1572864 | tf_op jit(solution)/shard_map/reduce_strips/pallas_call | solution.py:243
  180.6 1.3 collective-permute-start.3
  181.9 1.3 fusion.3
  183.2 1.5 collective-permute-done.3
  184.7 0.9 add.104
  185.7 0.0 all-to-all-done.2
  185.7 1.5 slice_bitcast_fusion.4
  187.2 0.6 gather_fusion.4
  187.8 0.1 select_convert_fusion
  187.9 0.6 gather_fusion.3
  188.5 0.1 select_convert_fusion.1
  188.7 0.6 gather_fusion.2
  189.3 0.1 select_convert_fusion.2
  189.4 1.9 add_convert_fusion
  191.3 10.4 %all-to-all-start.3 = ((bf16[16,2,2,8,1024]{4,3,1,2,0:T(8,128)(2,1)}), bf16[16,2,2,8,1024]{4,3,1,2,0:T(8,128)(2,1)S(1)}, u32[]{:S(2)}, u32[]{:S(2)}) async-start(bf16[16,2,2,8,1024]{4,3,1,2,0:T(8,128)(2,1)} %add_convert_fusion), calls=%async_computation.3 | async-start | bytes 2097152 | tf_op jit(solution)/shard_map/all_to_all | solution.py:258
  201.7 0.1 fusion.7
  201.8 0.4 collective-permute-start.5
  202.2 1.4 collective-permute-start.4
  203.6 28.7 %all-to-all-done.3 = bf16[16,2,2,8,1024]{4,3,1,2,0:T(8,128)(2,1)S(1)} async-done(((bf16[16,2,2,8,1024]{4,3,1,2,0:T(8,128)(2,1)}), bf16[16,2,2,8,1024]{4,3,1,2,0:T(8,128)(2,1)S(1)}, u32[]{:S(2)}, u32[]{:S(2)}) %all-to-all-start.3) | async-done | bytes 1048608 | tf_op jit(solution)/shard_map/all_to_all | solution.py:258
  232.2 0.2 convert_bitcast_fusion
  232.5 0.1 copy.43
  232.6 0.0 collective-permute-done.5
  232.6 0.0 collective-permute-done.4
  232.6 1.4 copy-done.1
  234.1 0.6 fusion.2
  234.7 1.0 slice_bitcast_fusion
  (22 shorter events, 0.1 us)
Async XLA Ops:
  0.6 12.3 %copy-start = (s32[3,2,16]{2,1,0:T(2,128)S(1)}, s32[3,2,16]{2,1,0:T(2,128)}, u32[]{:S(2)}) copy-start(s32[3,2,16]{2,1,0:T(2,128)} %param.16) | copy-start | bytes 1156
  3.9 9.1 %copy-start.5 = (s32[3,2,16]{2,1,0:T(2,128)S(1)}, s32[3,2,16]{2,1,0:T(2,128)}, u32[]{:S(2)}) copy-start(s32[3,2,16]{2,1,0:T(2,128)} %param.15) | copy-start | bytes 1156
  3.9 9.4 %copy-start.3 = (s32[256,128]{1,0:T(8,128)S(1)}, s32[256,128]{1,0:T(8,128)}, u32[]{:S(2)}) copy-start(s32[256,128]{1,0:T(8,128)} %param.14) | copy-start | bytes 393220
  3.9 10.2 %copy-start.4 = (s32[2]{0:T(128)S(1)}, s32[2]{0:T(128)}, u32[]{:S(2)}) copy-start(s32[2]{0:T(128)} %param.17) | copy-start | bytes 28
  3.9 37.2 %all-to-all-start = ((bf16[16,2,8,2048]{3,2,1,0:T(8,128)(2,1)}), bf16[16,2,8,2048]{3,2,1,0:T(8,128)(2,1)S(1)}, u32[]{:S(2)}, u32[]{:S(2)}) async-start(bf16[16,2,8,2048]{3,2,1,0:T(8,128)(2,1)} %bitcast.77), calls=%async_computation | async-start | bytes 2097152 | tf_op jit(solution)/shard_map/all_to_all | solution.py:258
  11.5 93.9 %collective-permute-start = (bf16[128,2048]{1,0:T(8,128)(2,1)}, bf16[128,2048]{1,0:T(8,128)(2,1)}, u32[]{:S(2)}, u32[]{:S(2)}) collective-permute-start(bf16[128,2048]{1,0:T(8,128)(2,1)} %get-tuple-element.35), channel_id=1, source_target_pairs={{0,1},{1,2},{2,3},{3,4},{4,5},{5,6},{6,7},{7,8},{8,9},{9,10},{10,1... | collective-permute-start | bytes 1572872 | tf_op jit(solution)/shard_map/ppermute | solution.py:298
  12.9 92.4 %collective-permute-start.1 = (bf16[128,2048]{1,0:T(8,128)(2,1)S(1)}, bf16[128,2048]{1,0:T(8,128)(2,1)}, u32[]{:S(2)}, u32[]{:S(2)}) collective-permute-start(bf16[128,2048]{1,0:T(8,128)(2,1)S(1)} %get-tuple-element.34), channel_id=1, source_target_pairs={{1,0},{2,1},{3,2},{4,3},{5,4},{6,5},{7,6},{8,7},{9,8},{10,9},{11,1... | collective-permute-start | bytes 1572872 | tf_op jit(solution)/shard_map/ppermute | solution.py:299
  43.2 60.8 %all-to-all-start.1 = ((bf16[16,3,8,2048]{3,2,1,0:T(8,128)(2,1)}), bf16[16,3,8,2048]{3,2,1,0:T(8,128)(2,1)S(1)}, u32[]{:S(2)}, u32[]{:S(2)}) async-start(bf16[16,3,8,2048]{3,2,1,0:T(8,128)(2,1)} %broadcast_select_fusion), calls=%async_computation.1 | async-start | bytes 3145728 | tf_op jit(solution)/shard_map/all_to_all | solution.py:258
  48.6 3.4 %collective-permute-start.2 = (bf16[2,8,2048]{2,1,0:T(8,128)(2,1)S(1)}, bf16[2,8,2048]{2,1,0:T(8,128)(2,1)S(1)}, u32[]{:S(2)}, u32[]{:S(2)}) collective-permute-start(bf16[2,8,2048]{2,1,0:T(8,128)(2,1)S(1)} %broadcast_select_fusion.1), channel_id=1, source_target_pairs={{0,16},{16,0},{1,17},{17,1},{2,18},{18,2},{3,19},{19,3},{4,20},{20... | collective-permute-start | bytes 196616 | tf_op jit(solution)/shard_map/ppermute | solution.py:292
  133.3 52.4 %all-to-all-start.2 = ((bf16[16,3,2,8,1024]{4,3,2,1,0:T(8,128)(2,1)}), bf16[16,3,2,8,1024]{4,3,2,1,0:T(8,128)(2,1)}, u32[]{:S(2)}, u32[]{:S(2)}) async-start(bf16[16,3,2,8,1024]{4,3,2,1,0:T(8,128)(2,1)} %slice.98), calls=%async_computation.2 | async-start | bytes 3145728 | tf_op jit(solution)/shard_map/all_to_all | solution.py:258
  180.6 4.1 %collective-permute-start.3 = (f32[2,2,8,1024]{3,2,1,0:T(8,128)}, f32[2,2,8,1024]{3,2,1,0:T(8,128)S(1)}, u32[]{:S(2)}, u32[]{:S(2)}) collective-permute-start(f32[2,2,8,1024]{3,2,1,0:T(8,128)} %bitcast.94), channel_id=1, source_target_pairs={{0,16},{16,0},{1,17},{17,1},{2,18},{18,2},{3,19},{19,3},{4,20},{20... | collective-permute-start | bytes 393224 | tf_op jit(solution)/shard_map/ppermute | solution.py:315
  191.3 10.4 %copy-start.2 = (bf16[2,256,1024]{2,1,0:T(8,128)(2,1)S(1)}, bf16[2,256,1024]{2,1,0:T(8,128)(2,1)}, u32[]{:S(2)}) copy-start(bf16[2,256,1024]{2,1,0:T(8,128)(2,1)} %get-tuple-element.14) | copy-start | bytes 3145732
  191.3 41.0 %all-to-all-start.3 = ((bf16[16,2,2,8,1024]{4,3,1,2,0:T(8,128)(2,1)}), bf16[16,2,2,8,1024]{4,3,1,2,0:T(8,128)(2,1)S(1)}, u32[]{:S(2)}, u32[]{:S(2)}) async-start(bf16[16,2,2,8,1024]{4,3,1,2,0:T(8,128)(2,1)} %add_convert_fusion), calls=%async_computation.3 | async-start | bytes 2097152 | tf_op jit(solution)/shard_map/all_to_all | solution.py:258
  201.8 30.9 %collective-permute-start.5 = (bf16[2,128,1024]{2,1,0:T(8,128)(2,1)S(1)}, bf16[2,128,1024]{2,1,0:T(8,128)(2,1)S(1)}, u32[]{:S(2)}, u32[]{:S(2)}) collective-permute-start(bf16[2,128,1024]{2,1,0:T(8,128)(2,1)S(1)} %get-tuple-element.33), channel_id=1, source_target_pairs={{1,0},{2,1},{3,2},{4,3},{5,4},{6,5},{7,6},{8,7},{9,8},{10,9},{11,1... | collective-permute-start | bytes 1572872 | tf_op jit(solution)/shard_map/ppermute | solution.py:305
  202.2 30.4 %collective-permute-start.4 = (bf16[2,128,1024]{2,1,0:T(8,128)(2,1)S(1)}, bf16[2,128,1024]{2,1,0:T(8,128)(2,1)S(1)}, u32[]{:S(2)}, u32[]{:S(2)}) collective-permute-start(bf16[2,128,1024]{2,1,0:T(8,128)(2,1)S(1)} %get-tuple-element.32), channel_id=1, source_target_pairs={{0,1},{1,2},{2,3},{3,4},{4,5},{5,6},{6,7},{7,8},{8,9},{9,10},{10,1... | collective-permute-start | bytes 1572872 | tf_op jit(solution)/shard_map/ppermute | solution.py:306
  232.5 1.6 copy-start.1

commit v3 on v2

--- a/solution.py
+++ b/solution.py
@@ -164,19 +164,54 @@
     return flag, me + 2**bit - 2 * 2**bit * flag
 
 
-def greet(me, levels):
+def greet(me, cols):
     barrier = pltpu.get_barrier_semaphore()
-    for bit in range(levels):
-        pl.semaphore_signal(barrier, inc=1, device_id={"col": partner_of(me, bit)[1]})
-    pl.semaphore_wait(barrier, levels)
-
-
-def gather_kernel(levels, strip_ref, all_ref, send_sem, recv_sem):
+
+    def hello(step, carry):
+        pl.semaphore_signal(barrier, inc=1, device_id={"col": (me + step) % cols})
+        return carry
+
+    lax.fori_loop(1, cols, hello, 0)
+    pl.semaphore_wait(barrier, cols - 1)
+
+
+def bulk_copy(me, cols, step, from_ref, to_ref, sems):
+    other = (me + step) % cols
+    return pltpu.make_async_remote_copy(
+        src_ref=from_ref.at[other],
+        dst_ref=to_ref.at[me],
+        send_sem=sems[0].at[step],
+        recv_sem=sems[1].at[step],
+        device_id={"col": other},
+    )
+
+
+def bulk_start(me, cols, lower, upper, from_ref, to_ref, sems):
+    def send(step, carry):
+        bulk_copy(me, cols, step, from_ref, to_ref, sems).start()
+        return carry
+
+    lax.fori_loop(lower, upper, send, 0)
+
+
+def bulk_wait(me, cols, from_ref, to_ref, sems):
+    def finish(step, carry):
+        bulk_copy(me, cols, step, from_ref, to_ref, sems).wait()
+        return carry
+
+    lax.fori_loop(1, cols, finish, 0)
+
+
+def groups_of(cols, levels):
+    return [1 + (cols - 1) * i // levels for i in range(levels + 1)]
+
+
+def gather_kernel(cols, levels, strip_ref, from_ref, all_ref, to_ref, send_sem, recv_sem, *sems):
     me = lax.axis_index("col")
-    greet(me, levels)
+    greet(me, cols)
     flags = [partner_of(me, levels - 1 - d)[0] for d in range(levels)]
-    pick = pl.ds
-    here = tuple(pick(flag, 1) for flag in flags)
+    here = tuple(pl.ds(flag, 1) for flag in flags)
+    bounds = groups_of(cols, levels)
     all_ref[here] = strip_ref[...].reshape((1,) * levels + strip_ref.shape)
     for dim in range(levels):
         region = (slice(None),) * dim + here[dim:]
@@ -188,29 +223,40 @@
             device_id={"col": partner_of(me, levels - 1 - dim)[1]},
         )
         copy.start()
+        bulk_start(me, cols, bounds[dim], bounds[dim + 1], from_ref, to_ref, sems)
+        if dim == 0:
+            to_ref[me] = from_ref[me]
         copy.wait()
-
-
-def gather_strips(strip, cols):
+    bulk_wait(me, cols, from_ref, to_ref, sems)
+
+
+def gather_exchange(strip, pieces):
+    cols = pieces.shape[0]
     levels = cols.bit_length() - 1
     vmem = pl.BlockSpec(memory_space=pltpu.VMEM)
-    out = pl.pallas_call(
-        functools.partial(gather_kernel, levels),
-        out_shape=jax.ShapeDtypeStruct((2,) * levels + strip.shape, strip.dtype),
-        in_specs=[vmem],
-        out_specs=vmem,
-        scratch_shapes=[pltpu.SemaphoreType.DMA((levels,)), pltpu.SemaphoreType.DMA((levels,))],
+    out, landed = pl.pallas_call(
+        functools.partial(gather_kernel, cols, levels),
+        out_shape=[
+            jax.ShapeDtypeStruct((2,) * levels + strip.shape, strip.dtype),
+            jax.ShapeDtypeStruct(pieces.shape, pieces.dtype),
+        ],
+        in_specs=[vmem, vmem],
+        out_specs=[vmem, vmem],
+        scratch_shapes=[pltpu.SemaphoreType.DMA((levels,))] * 2 + [pltpu.SemaphoreType.DMA((cols,))] * 2,
         compiler_params=pltpu.CompilerParams(collective_id=1, has_side_effects=True),
-        cost_estimate=pl.CostEstimate(flops=2 * 10**10, bytes_accessed=3 * cols * strip.size, transcendentals=0),
-        name="gather_strips",
-    )(strip)
-    return out.reshape((cols,) + strip.shape)
-
-
-def reduce_kernel(levels, parts_ref, sum_ref, *scratch):
-    landing, sums, (send_sem, recv_sem) = scratch[:levels], scratch[levels : 2 * levels - 1], scratch[2 * levels - 1 :]
+        cost_estimate=pl.CostEstimate(flops=3 * 10**10, bytes_accessed=4 * pieces.size, transcendentals=0),
+        name="gather_exchange",
+    )(strip, pieces)
+    return out.reshape((cols,) + strip.shape), landed
+
+
+def reduce_kernel(cols, levels, parts_ref, from_ref, sum_ref, to_ref, *scratch):
+    landing, sums = scratch[:levels], scratch[levels : 2 * levels - 1]
+    send_sem, recv_sem = scratch[2 * levels - 1 : 2 * levels + 1]
+    sems = scratch[2 * levels + 1 :]
     me = lax.axis_index("col")
-    greet(me, levels)
+    greet(me, cols)
+    bounds = groups_of(cols, levels)
     source = parts_ref
     for bit in range(levels):
         dim = levels - 1 - bit
@@ -225,6 +271,9 @@
             device_id={"col": partner},
         )
         copy.start()
+        bulk_start(me, cols, bounds[bit], bounds[bit + 1], from_ref, to_ref, sems)
+        if bit == 0:
+            to_ref[me] = from_ref[me]
         copy.wait()
         mine = source[lead + (pl.ds(flag, 1),) + tail]
         total = mine.astype(jnp.float32) + landing[bit][...].astype(jnp.float32)
@@ -233,25 +282,29 @@
             source[...] = total
         else:
             sum_ref[...] = total.reshape(sum_ref.shape)
-
-
-def reduce_strips(parts):
+    bulk_wait(me, cols, from_ref, to_ref, sems)
+
+
+def reduce_exchange(parts, pieces):
     cols, rows, width = parts.shape
     levels = cols.bit_length() - 1
     vmem = pl.BlockSpec(memory_space=pltpu.VMEM)
     shapes = [(2,) * (levels - 1 - bit) + (1,) * (bit + 1) + (rows, width) for bit in range(levels)]
     return pl.pallas_call(
-        functools.partial(reduce_kernel, levels),
-        out_shape=jax.ShapeDtypeStruct((rows, width), jnp.float32),
-        in_specs=[vmem],
-        out_specs=vmem,
+        functools.partial(reduce_kernel, cols, levels),
+        out_shape=[
+            jax.ShapeDtypeStruct((rows, width), jnp.float32),
+            jax.ShapeDtypeStruct(pieces.shape, pieces.dtype),
+        ],
+        in_specs=[vmem, vmem],
+        out_specs=[vmem, vmem],
         scratch_shapes=[pltpu.VMEM(shape, jnp.float32 if bit else parts.dtype) for bit, shape in enumerate(shapes)]
         + [pltpu.VMEM(shape, jnp.float32) for shape in shapes[:-1]]
-        + [pltpu.SemaphoreType.DMA((levels,)), pltpu.SemaphoreType.DMA((levels,))],
+        + [pltpu.SemaphoreType.DMA((levels,))] * 2 + [pltpu.SemaphoreType.DMA((cols,))] * 2,
         compiler_params=pltpu.CompilerParams(collective_id=2, has_side_effects=True),
-        cost_estimate=pl.CostEstimate(flops=2 * 10**10, bytes_accessed=3 * parts.size, transcendentals=0),
-        name="reduce_strips",
-    )(parts.reshape((2,) * levels + (rows, width)))
+        cost_estimate=pl.CostEstimate(flops=3 * 10**10, bytes_accessed=4 * pieces.size, transcendentals=0),
+        name="reduce_exchange",
+    )(parts.reshape((2,) * levels + (rows, width)), pieces)
 
 
 def exchange(pieces):
@@ -291,10 +344,13 @@
             ring = [(i, (i + step) % bands) for i in range(bands)]
             other = lax.ppermute(global_strips, "row", ring)
             chosen = jnp.where((owners == (band - step) % bands)[:, None, None], other, chosen)
-        shared = gather_strips(chosen.reshape(NGLOBAL * rows, 2 * part), cols)
+        sent = jnp.take(strips, wanted_ids, axis=0).reshape(cols, NMATCH, rows, 2 * part)
+        shared, fetched = gather_exchange(
+            chosen.reshape(NGLOBAL * rows, 2 * part), sent.reshape(cols, NMATCH * rows, 2 * part)
+        )
         shared = shared.reshape(cols, NGLOBAL, rows, 2 * part).swapaxes(0, 1).reshape(NGLOBAL * BLOCK, 2 * part)
-        sent = jnp.take(strips, wanted_ids, axis=0).reshape(cols, NMATCH, rows, 2 * part)
-        fetched = exchange(sent).swapaxes(0, 1).reshape(NMATCH * BLOCK, 2 * part)
+        fetched = fetched.reshape(cols, NMATCH, rows, 2 * part)
+        fetched = fetched.swapaxes(0, 1).reshape(NMATCH * BLOCK, 2 * part)
         before = lax.ppermute(both[tokens_here - BLOCK :], ("row", "col"), up)
         after = lax.ppermute(both[:BLOCK], ("row", "col"), down)
         att, qgrad, own, rims, far = attention(
@@ -306,8 +362,11 @@
         from_last = lax.ppermute(rims[:, BLOCK:], ("row", "col"), up)
         slots = NGLOBAL + NMATCH
         pieces = far.reshape(2, slots, cols, rows, part).transpose(2, 1, 0, 3, 4)
-        landed = exchange(pieces[:, NGLOBAL:])
-        strips_sum = reduce_strips(pieces[:, :NGLOBAL].reshape(cols, NGLOBAL * 2 * rows, part))
+        strips_sum, landed = reduce_exchange(
+            pieces[:, :NGLOBAL].reshape(cols, NGLOBAL * 2 * rows, part),
+            pieces[:, NGLOBAL:].reshape(cols, NMATCH * 2 * rows, part),
+        )
+        landed = landed.reshape(cols, NMATCH, 2, rows, part)
         band_sum = strips_sum.reshape(NGLOBAL, 2, rows, part)
         global_sum = band_sum
         for step in range(1, bands):

time: 237 us -> 232 us (0.979)
  Pallas kernels: 115 us -> 126 us
  starting transfers between devices: 32.2 us -> 21.3 us
  waiting for transfers between devices: 58.6 us -> 55 us
    pallas_call x2, Pallas kernels: 90.5 us -> 101 us  [the longest x1 59.5 us: reduce_exchange(): pl.pallas_call(functools.partial(reduce_kernel, cols, levels), out_shape=...]
    all_to_all x4 -> x2, starting transfers between devices: 26.3 us -> 15.7 us  [exchange(): lax.all_to_all(pieces, 'col', split_axis=0, concat_axis=0, tiled=True)]
    reshape x0 -> x1, local copies, waits for them, and re-layouts: none -> 2.88 us  [body(): fetched = fetched.reshape(cols, NMATCH, rows, 2 * part)]
    all_to_all x4 -> x2, waiting for transfers between devices: 55 us -> 53.8 us  [exchange(): lax.all_to_all(pieces, 'col', split_axis=0, concat_axis=0, tiled=True)]
  transfers between devices with their start and end apart: 10 -> 8, of which waited for: 4 -> 4; matrix products, arithmetic and copies ran while one was open for 6% -> 6% of each run, Pallas kernels for 38% -> 18%
where the time goes in v3:
time: 232 us
  Pallas kernels  126 us (54%)
  waiting for transfers between devices  55 us (24%)
  local copies, waits for them, and re-layouts  21.4 us (9%)
  starting transfers between devices  21.3 us (9%)
  other arithmetic  6.9 us (3%)
    pallas_call x1, Pallas kernels, reduce_exchange(): pl.pallas_call(functools.partial(reduce_kernel, cols, levels), out_shape=...  59.5 us
    all_to_all x2, waiting for transfers between devices, exchange(): lax.all_to_all(pieces, 'col', split_axis=0, concat_axis=0, tiled=True)  53.8 us
    pallas_call x1, Pallas kernels, gather_exchange(): pl.pallas_call(functools.partial(gather_kernel, cols, levels), out_shape=...  41.9 us
    pallas_call x1, Pallas kernels, attention(): pl.pallas_call(functools.partial(attention_kernel, blocks), grid=(pairs,)...  24.5 us
    all_to_all x2, starting transfers between devices, exchange(): lax.all_to_all(pieces, 'col', split_axis=0, concat_axis=0, tiled=True)  15.7 us
  transfers between devices with their start and end apart: 8, of which 4 were waited for; matrix products, arithmetic and copies ran while one was open for 6% of the time, Pallas kernels for 18%

profile of v3, /device:TPU:9, one launch (start us, length us, event | category | flops | bytes accessed | tf_op | source)
XLA Modules:
  0.0 231.5 jit_solution(976936224198349086)
XLA Ops:
  0.6 0.0 copy-start
  0.6 1.1 constant_dynamic-update-slice_fusion.1
  1.7 1.1 constant_dynamic-update-slice_fusion
  2.8 1.1 copy.59
  3.9 6.7 %all-to-all-start = ((bf16[16,2,8,2048]{3,2,1,0:T(8,128)(2,1)}), bf16[16,2,8,2048]{3,2,1,0:T(8,128)(2,1)S(1)}, u32[]{:S(2)}, u32[]{:S(2)}) async-start(bf16[16,2,8,2048]{3,2,1,0:T(8,128)(2,1)} %bitcast.84), calls=%async_computation | async-start | bytes 2097152 | tf_op jit(solution)/shard_map/all_to_all | solution.py:311
  10.6 0.9 fusion.8
  11.5 1.5 collective-permute-start
  12.9 0.0 collective-permute-start.1
  12.9 0.0 copy-done
  12.9 0.0 copy-done.7
  13.0 0.0 copy-done.6
  13.1 0.1 copy.40
  13.1 0.1 reshape.197
  13.2 0.1 copy.39
  13.3 0.0 copy-done.5
  13.3 0.8 copy.43
  14.1 0.1 select_reduce_fusion.1
  14.2 0.6 fusion.9
  14.8 1.3 fusion.3
  16.1 0.1 iota_compare_fusion.3
  16.2 0.1 iota_compare_fusion.1
  16.3 24.8 %all-to-all-done = bf16[16,2,8,2048]{3,2,1,0:T(8,128)(2,1)S(1)} async-done(((bf16[16,2,8,2048]{3,2,1,0:T(8,128)(2,1)}), bf16[16,2,8,2048]{3,2,1,0:T(8,128)(2,1)S(1)}, u32[]{:S(2)}, u32[]{:S(2)}) %all-to-all-start) | async-done | bytes 1048608 | tf_op jit(solution)/shard_map/all_to_all | solution.py:311
  41.1 0.5 gather_fusion
  41.7 0.1 broadcast_select_fusion
  41.7 1.2 collective-permute-start.2
  43.0 0.7 gather_fusion.1
  43.7 1.4 bitcast_select_fusion.from_ref
  45.0 0.8 collective-permute-done.2
  45.9 0.7 select_bitcast_fusion.strip_ref
  46.6 41.9 %gather_exchange.1 = (bf16[2,2,2,2,16,2048]{5,4,3,2,1,0:T(8,128)(2,1)}, bf16[16,24,2048]{2,1,0:T(8,128)(2,1)}) custom-call(bf16[16,2048]{1,0:T(8,128)(2,1)} %select_bitcast_fusion.strip_ref, bf16[16,24,2048]{2,1,0:T(8,128)(2,1)} %bitcast_select_fusion.from_ref), custom_call_target="tpu_custom_call" | custom-call | flops 30000001024 | bytes 3145728 | tf_op jit(solution)/shard_map/gather_exchange/pallas_call | solution.py:237
  88.5 0.0 copy-start.3
  88.5 2.9 %copy.42 = bf16[16,3,8,2048]{3,2,0,1:T(8,128)(2,1)} copy(bf16[16,3,8,2048]{3,2,1,0:T(8,128)(2,1)} %bitcast.98) | data formatting | bytes 3145728 | tf_op jit(solution)/shard_map/reshape | solution.py:352
  91.4 0.0 copy-done.3
  91.4 1.2 copy.41
  92.6 0.0 collective-permute-done.kp_ref.vp_ref
  92.6 0.0 collective-permute-done.1.kn_ref.vn_ref
  92.6 24.5 %block_attention.1 = (bf16[256,1024]{1,0:T(8,128)(2,1)}, bf16[256,1024]{1,0:T(8,128)(2,1)}, f32[2,256,1024]{2,1,0:T(8,128)}, bf16[2,256,1024]{2,1,0:T(8,128)(2,1)}, bf16[2,640,1024]{2,1,0:T(8,128)(2,1)}) custom-call(bf16[256,1024]{1,0:T(8,128)(2,1)} %q_ref.1, bf16[256,1024]{1,0:T(8,128)(2,1)} %g_ref.1, bf16[256,1024]{1,0:T(8,128)(2,1)} %ko_ref.1, ...), custom_call_target="tpu_custom_call" | custom-call | flops 3758096384 | bytes 4194304 | tf_op jit(solution)/shard_map/block_attention/pallas_call | solution.py:136
  117.1 2.0 copy.58
  119.1 1.3 slice.99
  120.5 1.1 slice.98
  121.6 59.5 %reduce_exchange.1 = (f32[32,1024]{1,0:T(8,128)}, bf16[16,48,1024]{2,1,0:T(8,128)(2,1)}) custom-call(bf16[2,2,2,2,32,1024]{5,4,3,2,1,0:T(8,128)(2,1)} %bitcast.103, bf16[16,48,1024]{2,1,0:T(8,128)(2,1)} %bitcast.99), custom_call_target="tpu_custom_call" | custom-call | flops 30000001024 | bytes 3145728 | tf_op jit(solution)/shard_map/reduce_exchange/pallas_call | solution.py:293
  181.0 0.0 copy-start.4
  181.0 1.6 slice_bitcast_fusion.4
  182.6 1.3 collective-permute-start.3
  183.9 0.6 gather_fusion.4
  184.5 0.1 select_convert_fusion
  184.7 0.6 gather_fusion.3
  185.3 0.1 select_convert_fusion.1
  185.4 0.6 gather_fusion.2
  186.0 0.1 select_convert_fusion.2
  186.1 0.4 collective-permute-done.3
  186.5 1.9 add_convert_fusion
  188.4 9.1 %all-to-all-start.1 = ((bf16[16,2,2,8,1024]{4,3,1,2,0:T(8,128)(2,1)}), bf16[16,2,2,8,1024]{4,3,1,2,0:T(8,128)(2,1)S(1)}, u32[]{:S(2)}, u32[]{:S(2)}) async-start(bf16[16,2,2,8,1024]{4,3,1,2,0:T(8,128)(2,1)} %add_convert_fusion), calls=%async_computation.1 | async-start | bytes 2097152 | tf_op jit(solution)/shard_map/all_to_all | solution.py:311
  197.5 0.1 fusion.7
  197.6 1.5 collective-permute-start.4
  199.1 0.0 collective-permute-start.5
  199.1 28.9 %all-to-all-done.1 = bf16[16,2,2,8,1024]{4,3,1,2,0:T(8,128)(2,1)S(1)} async-done(((bf16[16,2,2,8,1024]{4,3,1,2,0:T(8,128)(2,1)}), bf16[16,2,2,8,1024]{4,3,1,2,0:T(8,128)(2,1)S(1)}, u32[]{:S(2)}, u32[]{:S(2)}) %all-to-all-start.1) | async-done | bytes 1048608 | tf_op jit(solution)/shard_map/all_to_all | solution.py:311
  228.0 0.2 convert_bitcast_fusion
  228.3 0.1 copy.45
  228.4 0.0 collective-permute-done.4
  228.4 0.0 collective-permute-done.5
  228.5 1.4 copy-done.1
  229.9 0.6 fusion.2
  230.5 1.0 slice_bitcast_fusion
  (23 shorter events, 0.1 us)
Async XLA Ops:
  0.6 12.3 %copy-start = (s32[3,2,16]{2,1,0:T(2,128)S(1)}, s32[3,2,16]{2,1,0:T(2,128)}, u32[]{:S(2)}) copy-start(s32[3,2,16]{2,1,0:T(2,128)} %param.16) | copy-start | bytes 1156
  3.9 9.1 %copy-start.7 = (s32[3,2,16]{2,1,0:T(2,128)S(1)}, s32[3,2,16]{2,1,0:T(2,128)}, u32[]{:S(2)}) copy-start(s32[3,2,16]{2,1,0:T(2,128)} %param.15) | copy-start | bytes 1156
  3.9 9.1 %copy-start.6 = (s32[2]{0:T(128)S(1)}, s32[2]{0:T(128)}, u32[]{:S(2)}) copy-start(s32[2]{0:T(128)} %param.17) | copy-start | bytes 28
  3.9 9.4 %copy-start.5 = (s32[256,128]{1,0:T(8,128)S(1)}, s32[256,128]{1,0:T(8,128)}, u32[]{:S(2)}) copy-start(s32[256,128]{1,0:T(8,128)} %param.14) | copy-start | bytes 393220
  3.9 37.2 %all-to-all-start = ((bf16[16,2,8,2048]{3,2,1,0:T(8,128)(2,1)}), bf16[16,2,8,2048]{3,2,1,0:T(8,128)(2,1)S(1)}, u32[]{:S(2)}, u32[]{:S(2)}) async-start(bf16[16,2,8,2048]{3,2,1,0:T(8,128)(2,1)} %bitcast.84), calls=%async_computation | async-start | bytes 2097152 | tf_op jit(solution)/shard_map/all_to_all | solution.py:311
  11.5 81.1 %collective-permute-start = (bf16[128,2048]{1,0:T(8,128)(2,1)}, bf16[128,2048]{1,0:T(8,128)(2,1)}, u32[]{:S(2)}, u32[]{:S(2)}) collective-permute-start(bf16[128,2048]{1,0:T(8,128)(2,1)} %get-tuple-element.43), channel_id=1, source_target_pairs={{0,1},{1,2},{2,3},{3,4},{4,5},{5,6},{6,7},{7,8},{8,9},{9,10},{10,1... | collective-permute-start | bytes 1572872 | tf_op jit(solution)/shard_map/ppermute | solution.py:354
  12.9 79.6 %collective-permute-start.1 = (bf16[128,2048]{1,0:T(8,128)(2,1)S(1)}, bf16[128,2048]{1,0:T(8,128)(2,1)}, u32[]{:S(2)}, u32[]{:S(2)}) collective-permute-start(bf16[128,2048]{1,0:T(8,128)(2,1)S(1)} %get-tuple-element.42), channel_id=1, source_target_pairs={{1,0},{2,1},{3,2},{4,3},{5,4},{6,5},{7,6},{8,7},{9,8},{10,9},{11,1... | collective-permute-start | bytes 1572872 | tf_op jit(solution)/shard_map/ppermute | solution.py:355
  41.7 4.1 %collective-permute-start.2 = (bf16[2,8,2048]{2,1,0:T(8,128)(2,1)S(1)}, bf16[2,8,2048]{2,1,0:T(8,128)(2,1)S(1)}, u32[]{:S(2)}, u32[]{:S(2)}) collective-permute-start(bf16[2,8,2048]{2,1,0:T(8,128)(2,1)S(1)} %broadcast_select_fusion), channel_id=1, source_target_pairs={{0,16},{16,0},{1,17},{17,1},{2,18},{18,2},{3,19},{19,3},{4,20},{20... | collective-permute-start | bytes 196616 | tf_op jit(solution)/shard_map/ppermute | solution.py:345
  88.5 2.9 %copy-start.3 = (bf16[2,2,2,2,16,2048]{5,4,3,2,1,0:T(8,128)(2,1)S(1)}, bf16[2,2,2,2,16,2048]{5,4,3,2,1,0:T(8,128)(2,1)}, u32[]{:S(2)}) copy-start(bf16[2,2,2,2,16,2048]{5,4,3,2,1,0:T(8,128)(2,1)} %get-tuple-element.14) | copy-start | bytes 3145732
  181.0 1.6 copy-start.4
  182.6 3.9 %collective-permute-start.3 = (f32[2,2,8,1024]{3,2,1,0:T(8,128)S(1)}, f32[2,2,8,1024]{3,2,1,0:T(8,128)S(1)}, u32[]{:S(2)}, u32[]{:S(2)}) collective-permute-start(f32[2,2,8,1024]{3,2,1,0:T(8,128)S(1)} %bitcast.104), channel_id=1, source_target_pairs={{0,16},{16,0},{1,17},{17,1},{2,18},{18,2},{3,19},{19,3},{4,20},{20... | collective-permute-start | bytes 393224 | tf_op jit(solution)/shard_map/ppermute | solution.py:374
  188.4 9.1 %copy-start.2 = (bf16[2,256,1024]{2,1,0:T(8,128)(2,1)S(1)}, bf16[2,256,1024]{2,1,0:T(8,128)(2,1)}, u32[]{:S(2)}) copy-start(bf16[2,256,1024]{2,1,0:T(8,128)(2,1)} %get-tuple-element.22) | copy-start | bytes 3145732
  188.4 39.6 %all-to-all-start.1 = ((bf16[16,2,2,8,1024]{4,3,1,2,0:T(8,128)(2,1)}), bf16[16,2,2,8,1024]{4,3,1,2,0:T(8,128)(2,1)S(1)}, u32[]{:S(2)}, u32[]{:S(2)}) async-start(bf16[16,2,2,8,1024]{4,3,1,2,0:T(8,128)(2,1)} %add_convert_fusion), calls=%async_computation.1 | async-start | bytes 2097152 | tf_op jit(solution)/shard_map/all_to_all | solution.py:311
  197.6 30.9 %collective-permute-start.4 = (bf16[2,128,1024]{2,1,0:T(8,128)(2,1)S(1)}, bf16[2,128,1024]{2,1,0:T(8,128)(2,1)S(1)}, u32[]{:S(2)}, u32[]{:S(2)}) collective-permute-start(bf16[2,128,1024]{2,1,0:T(8,128)(2,1)S(1)} %get-tuple-element.40), channel_id=1, source_target_pairs={{0,1},{1,2},{2,3},{3,4},{4,5},{5,6},{6,7},{7,8},{8,9},{9,10},{10,1... | collective-permute-start | bytes 1572872 | tf_op jit(solution)/shard_map/ppermute | solution.py:362
  199.1 29.4 %collective-permute-start.5 = (bf16[2,128,1024]{2,1,0:T(8,128)(2,1)S(1)}, bf16[2,128,1024]{2,1,0:T(8,128)(2,1)S(1)}, u32[]{:S(2)}, u32[]{:S(2)}) collective-permute-start(bf16[2,128,1024]{2,1,0:T(8,128)(2,1)S(1)} %get-tuple-element.41), channel_id=1, source_target_pairs={{1,0},{2,1},{3,2},{4,3},{5,4},{6,5},{7,6},{8,7},{9,8},{10,9},{11,1... | collective-permute-start | bytes 1572872 | tf_op jit(solution)/shard_map/ppermute | solution.py:361
  228.3 1.6 copy-start.1

commit v4 on v3

--- a/solution.py
+++ b/solution.py
@@ -175,7 +175,8 @@
     pl.semaphore_wait(barrier, cols - 1)
 
 
-def bulk_copy(me, cols, step, from_ref, to_ref, sems):
+def bulk_copy(me, cols, turn, from_ref, to_ref, sems):
+    step = (turn * (cols // 2 - 1)) % cols
     other = (me + step) % cols
     return pltpu.make_async_remote_copy(
         src_ref=from_ref.at[other],
@@ -204,6 +205,34 @@
 
 def groups_of(cols, levels):
     return [1 + (cols - 1) * i // levels for i in range(levels + 1)]
+
+
+def late_groups(cols, levels):
+    third, half = 1 + (cols - 1) // 3, 1 + (cols - 1) * 8 // 15
+    return [1, third, third] + [half] * (levels - 3) + [cols] * 1
+
+
+def exchange_kernel(cols, from_ref, to_ref, *sems):
+    me = lax.axis_index("col")
+    greet(me, cols)
+    bulk_start(me, cols, 1, cols, from_ref, to_ref, sems)
+    to_ref[me] = from_ref[me]
+    bulk_wait(me, cols, from_ref, to_ref, sems)
+
+
+def direct_exchange(pieces, number):
+    cols = pieces.shape[0]
+    vmem = pl.BlockSpec(memory_space=pltpu.VMEM)
+    return pl.pallas_call(
+        functools.partial(exchange_kernel, cols),
+        out_shape=jax.ShapeDtypeStruct(pieces.shape, pieces.dtype),
+        in_specs=[vmem],
+        out_specs=vmem,
+        scratch_shapes=[pltpu.SemaphoreType.DMA((cols,))] * 2,
+        compiler_params=pltpu.CompilerParams(collective_id=number, has_side_effects=True),
+        cost_estimate=pl.CostEstimate(flops=3 * 10**10, bytes_accessed=4 * pieces.size, transcendentals=0),
+        name="direct_exchange",
+    )(pieces)
 
 
 def gather_kernel(cols, levels, strip_ref, from_ref, all_ref, to_ref, send_sem, recv_sem, *sems):
@@ -256,7 +285,7 @@
     sems = scratch[2 * levels + 1 :]
     me = lax.axis_index("col")
     greet(me, cols)
-    bounds = groups_of(cols, levels)
+    bounds = late_groups(cols, levels)
     source = parts_ref
     for bit in range(levels):
         dim = levels - 1 - bit
@@ -279,7 +308,7 @@
         total = mine.astype(jnp.float32) + landing[bit][...].astype(jnp.float32)
         if bit < levels - 1:
             source = sums[bit]
-            source[...] = total
+            source[...] = total.astype(source.dtype)
         else:
             sum_ref[...] = total.reshape(sum_ref.shape)
     bulk_wait(me, cols, from_ref, to_ref, sems)
@@ -298,17 +327,13 @@
         ],
         in_specs=[vmem, vmem],
         out_specs=[vmem, vmem],
-        scratch_shapes=[pltpu.VMEM(shape, jnp.float32 if bit else parts.dtype) for bit, shape in enumerate(shapes)]
-        + [pltpu.VMEM(shape, jnp.float32) for shape in shapes[:-1]]
+        scratch_shapes=[pltpu.VMEM(shape, parts.dtype if bit < 2 else jnp.float32) for bit, shape in enumerate(shapes)]
+        + [pltpu.VMEM(shape, jnp.float32 if bit else parts.dtype) for bit, shape in enumerate(shapes[:-1])]
         + [pltpu.SemaphoreType.DMA((levels,))] * 2 + [pltpu.SemaphoreType.DMA((cols,))] * 2,
         compiler_params=pltpu.CompilerParams(collective_id=2, has_side_effects=True),
         cost_estimate=pl.CostEstimate(flops=3 * 10**10, bytes_accessed=4 * pieces.size, transcendentals=0),
         name="reduce_exchange",
     )(parts.reshape((2,) * levels + (rows, width)), pieces)
-
-
-def exchange(pieces):
-    return lax.all_to_all(pieces, "col", split_axis=0, concat_axis=0, tiled=True)
 
 
 def body(queries, key_rows, value_rows, out_grad, dropout_bits, partner, block_pick, global_blocks):
@@ -335,7 +360,8 @@
     for chunk in range(CHUNKS):
         lower, upper = chunk * part, (chunk + 1) * part
         both = jnp.concatenate([key_rows[:, lower:upper], value_rows[:, lower:upper]], 1)
-        spread = exchange(both.reshape(blocks, cols, rows, 2 * part).swapaxes(0, 1))
+        own_strips = both.reshape(blocks, cols, rows, 2 * part).swapaxes(0, 1)
+        spread = direct_exchange(own_strips.reshape(cols, blocks * rows, 2 * part), 3)
         strips = spread.reshape(cols * blocks, rows, 2 * part)
         global_strips = jnp.take(strips, global_ids, axis=0)
         owners = global_blocks // (cols * blocks)
@@ -382,7 +408,8 @@
         for g in range(NGLOBAL):
             mine = block_ids == global_blocks[g]
             returned = returned + jnp.where(mine[:, :, None, None, None], global_sum[g][None, None], 0.0)
-        home = exchange(returned.astype(jnp.bfloat16)).transpose(2, 1, 0, 3, 4).reshape(2, tokens_here, part)
+        home = direct_exchange(returned.astype(jnp.bfloat16).reshape(cols, blocks * 2 * rows, part), 4)
+        home = home.reshape(cols, blocks, 2, rows, part).transpose(2, 1, 0, 3, 4).reshape(2, tokens_here, part)
         total = own + home.astype(jnp.float32)
         room = ((0, 0), (0, tokens_here - BLOCK), (0, 0))
         total = total + jnp.pad(from_last.astype(jnp.float32), room)

time: 232 us -> 225 us (0.970)
  Pallas kernels: 126 us -> 181 us
  waiting for transfers between devices: 55 us -> 1.18 us
  starting transfers between devices: 21.3 us -> 4.31 us
  local copies, waits for them, and re-layouts: 21.4 us -> 25.5 us
    pallas_call x0 -> x2, Pallas kernels: none -> 59.1 us  [direct_exchange(): pl.pallas_call(functools.partial(exchange_kernel, cols), out_shape=jax.Sh...]
    all_to_all x2 -> x0, waiting for transfers between devices: 53.8 us -> none  [exchange(): lax.all_to_all(pieces, 'col', split_axis=0, concat_axis=0, tiled=True)]
    all_to_all x2 -> x0, starting transfers between devices: 15.7 us -> none  [exchange(): lax.all_to_all(pieces, 'col', split_axis=0, concat_axis=0, tiled=True)]
    pallas_call x1, Pallas kernels: 59.5 us -> 52.6 us  [reduce_exchange(): pl.pallas_call(functools.partial(reduce_kernel, cols, levels), out_shape=...]
    pallas_call x1, Pallas kernels: 41.9 us -> 45.1 us  [gather_exchange(): pl.pallas_call(functools.partial(gather_kernel, cols, levels), out_shape=...]
  transfers between devices with their start and end apart: 8 -> 6, of which waited for: 4 -> 1; matrix products, arithmetic and copies ran while one was open for 6% -> 8% of each run, Pallas kernels for 18% -> 34%
where the time goes in v4:
time: 225 us; the launch traced here: 222 us
  Pallas kernels  181 us (80%)
  local copies, waits for them, and re-layouts  25.5 us (11%)
  other arithmetic  9.16 us (4%)
  starting transfers between devices  4.31 us (2%)
    pallas_call x2, Pallas kernels, direct_exchange(): pl.pallas_call(functools.partial(exchange_kernel, cols), out_shape=jax.Sh...  59.1 us
    pallas_call x1, Pallas kernels, reduce_exchange(): pl.pallas_call(functools.partial(reduce_kernel, cols, levels), out_shape=...  52.6 us
    pallas_call x1, Pallas kernels, gather_exchange(): pl.pallas_call(functools.partial(gather_kernel, cols, levels), out_shape=...  45.1 us
    pallas_call x1, Pallas kernels, attention(): pl.pallas_call(functools.partial(attention_kernel, blocks), grid=(pairs,)...  24.5 us
  transfers between devices with their start and end apart: 6, of which 1 were waited for; matrix products, arithmetic and copies ran while one was open for 8% of the time, Pallas kernels for 34%

profile of v4, /device:TPU:9, one launch (start us, length us, event | category | flops | bytes accessed | tf_op | source)
XLA Modules:
  0.0 222.5 jit_solution(14907297084848409300)
XLA Ops:
  0.6 0.0 copy-start
  0.7 0.7 copy-done
  1.3 0.7 constant_dynamic-slice_fusion.1
  2.0 0.1 select_reduce_fusion.1
  2.1 1.1 constant_dynamic-update-slice_fusion.1
  3.2 1.1 constant_dynamic-update-slice_fusion
  4.3 1.0 copy.58
  5.4 29.0 %direct_exchange.2 = bf16[16,16,2048]{2,1,0:T(8,128)(2,1)} custom-call(bf16[16,16,2048]{2,1,0:T(8,128)(2,1)} %bitcast.136), custom_call_target="tpu_custom_call" | custom-call | flops 30000001024 | bytes 2097152 | tf_op jit(solution)/shard_map/direct_exchange/pallas_call | solution.py:226
  34.3 0.0 copy-done.7
  34.4 1.9 gather_fusion
  36.2 0.1 broadcast_select_fusion
  36.3 1.2 collective-permute-start.2
  37.6 0.9 fusion.13
  38.5 1.2 collective-permute-start
  39.7 0.8 collective-permute-start.1
  40.4 0.6 fusion.14
  41.0 0.1 copy.34
  41.1 0.1 reshape.215
  41.2 0.0 copy-done.1
  41.2 0.7 gather_fusion.1
  41.9 0.1 copy.33
  42.0 0.8 copy.37
  42.8 0.1 copy.40
  42.9 0.1 copy.41
  43.0 0.1 copy.38
  43.1 1.3 fusion.8
  44.4 0.1 copy.42
  44.5 0.1 copy.43
  44.6 1.4 bitcast_select_fusion.3.from_ref
  45.9 0.0 collective-permute-done.2
  45.9 0.7 select_bitcast_fusion.strip_ref
  46.6 45.1 %gather_exchange.1 = (bf16[2,2,2,2,16,2048]{5,4,3,2,1,0:T(8,128)(2,1)}, bf16[16,24,2048]{2,1,0:T(8,128)(2,1)}) custom-call(bf16[16,2048]{1,0:T(8,128)(2,1)} %select_bitcast_fusion.strip_ref, bf16[16,24,2048]{2,1,0:T(8,128)(2,1)} %bitcast_select_fusion.3.from_ref), custom_call_target="tpu_custom_call" | custom-call | flops 30000001024 | bytes 3145728 | tf_op jit(solution)/shard_map/gather_exchange/pallas_call | solution.py:266
  91.7 2.9 %copy.36 = bf16[16,3,8,2048]{3,2,0,1:T(8,128)(2,1)} copy(bf16[16,3,8,2048]{3,2,1,0:T(8,128)(2,1)} %bitcast.129) | data formatting | bytes 3145728 | tf_op jit(solution)/shard_map/reshape | solution.py:378
  94.6 1.1 copy.35
  95.8 0.0 collective-permute-done.kp_ref.vp_ref
  95.8 0.0 collective-permute-done.1.kn_ref.vn_ref
  95.8 24.5 %block_attention.1 = (bf16[256,1024]{1,0:T(8,128)(2,1)}, bf16[256,1024]{1,0:T(8,128)(2,1)}, f32[2,256,1024]{2,1,0:T(8,128)}, bf16[2,256,1024]{2,1,0:T(8,128)(2,1)}, bf16[2,640,1024]{2,1,0:T(8,128)(2,1)}) custom-call(bf16[256,1024]{1,0:T(8,128)(2,1)} %q_ref.1, bf16[256,1024]{1,0:T(8,128)(2,1)} %g_ref.1, bf16[256,1024]{1,0:T(8,128)(2,1)} %ko_ref.1, ...), custom_call_target="tpu_custom_call" | custom-call | flops 3758096384 | bytes 4194304 | tf_op jit(solution)/shard_map/block_attention/pallas_call | solution.py:136
  120.3 2.0 copy.57
  122.3 1.3 slice.99
  123.7 1.1 slice.98
  124.7 52.6 %reduce_exchange.1 = (f32[32,1024]{1,0:T(8,128)}, bf16[16,48,1024]{2,1,0:T(8,128)(2,1)}) custom-call(bf16[2,2,2,2,32,1024]{5,4,3,2,1,0:T(8,128)(2,1)} %bitcast.135, bf16[16,48,1024]{2,1,0:T(8,128)(2,1)} %bitcast.130), custom_call_target="tpu_custom_call" | custom-call | flops 30000001024 | bytes 3145728 | tf_op jit(solution)/shard_map/reduce_exchange/pallas_call | solution.py:322
  177.3 0.0 copy-start.5
  177.4 0.0 copy-start.3
  177.4 1.6 slice_bitcast_fusion.4
  179.0 0.6 collective-permute-start.3
  179.6 1.1 fusion.12
  180.6 0.0 collective-permute-start.4
  180.7 0.5 collective-permute-start.5
  181.2 0.6 gather_fusion.2
  181.7 0.1 select_convert_fusion.2
  181.9 0.6 gather_fusion.4
  182.5 0.1 select_convert_fusion
  182.6 0.6 gather_fusion.3
  183.2 0.1 select_convert_fusion.1
  183.4 1.2 collective-permute-done.3
  184.6 1.8 fusion.6.from_ref
  186.4 30.1 %direct_exchange.3 = bf16[16,32,1024]{2,1,0:T(8,128)(2,1)} custom-call(bf16[16,32,1024]{2,1,0:T(8,128)(2,1)} %fusion.6.from_ref), custom_call_target="tpu_custom_call" | custom-call | flops 30000001024 | bytes 2097152 | tf_op jit(solution)/shard_map/direct_exchange/pallas_call | solution.py:226
  216.5 1.5 convert_bitcast_fusion
  218.0 0.1 copy.44
  218.2 0.0 collective-permute-done.4
  218.2 0.0 collective-permute-done.5
  218.2 1.4 copy-done.2
  219.6 1.8 fusion.2
  221.5 1.0 slice_bitcast_fusion
  (32 shorter events, 0.2 us)
Async XLA Ops:
  0.6 0.7 copy-start
  5.4 29.0 %copy-start.7 = (s32[2]{0:T(128)S(1)}, s32[2]{0:T(128)}, u32[]{:S(2)}) copy-start(s32[2]{0:T(128)} %param.17) | copy-start | bytes 28
  34.3 6.9 %copy-start.1 = (bf16[16,16,2048]{2,1,0:T(8,128)(2,1)S(1)}, bf16[16,16,2048]{2,1,0:T(8,128)(2,1)}, u32[]{:S(2)}) copy-start(bf16[16,16,2048]{2,1,0:T(8,128)(2,1)} %direct_exchange.2) | copy-start | bytes 3145732
  36.3 9.6 %collective-permute-start.2 = (bf16[2,8,2048]{2,1,0:T(8,128)(2,1)S(1)}, bf16[2,8,2048]{2,1,0:T(8,128)(2,1)S(1)}, u32[]{:S(2)}, u32[]{:S(2)}) collective-permute-start(bf16[2,8,2048]{2,1,0:T(8,128)(2,1)S(1)} %broadcast_select_fusion), channel_id=1, source_target_pairs={{0,16},{16,0},{1,17},{17,1},{2,18},{18,2},{3,19},{19,3},{4,20},{20... | collective-permute-start | bytes 196616 | tf_op jit(solution)/shard_map/ppermute | solution.py:371
  38.5 3.5 %copy-start.6 = (s32[256,128]{1,0:T(8,128)S(1)}, s32[256,128]{1,0:T(8,128)}, u32[]{:S(2)}) copy-start(s32[256,128]{1,0:T(8,128)} %param.14) | copy-start | bytes 393220
  38.5 57.3 %collective-permute-start = (bf16[128,2048]{1,0:T(8,128)(2,1)}, bf16[128,2048]{1,0:T(8,128)(2,1)}, u32[]{:S(2)}, u32[]{:S(2)}) collective-permute-start(bf16[128,2048]{1,0:T(8,128)(2,1)} %get-tuple-element.43), channel_id=1, source_target_pairs={{0,1},{1,2},{2,3},{3,4},{4,5},{5,6},{6,7},{7,8},{8,9},{9,10},{10,1... | collective-permute-start | bytes 1572872 | tf_op jit(solution)/shard_map/ppermute | solution.py:380
  39.7 56.1 %collective-permute-start.1 = (bf16[128,2048]{1,0:T(8,128)(2,1)S(1)}, bf16[128,2048]{1,0:T(8,128)(2,1)}, u32[]{:S(2)}, u32[]{:S(2)}) collective-permute-start(bf16[128,2048]{1,0:T(8,128)(2,1)S(1)} %get-tuple-element.42), channel_id=1, source_target_pairs={{1,0},{2,1},{3,2},{4,3},{5,4},{6,5},{7,6},{8,7},{9,8},{10,9},{11,1... | collective-permute-start | bytes 1572872 | tf_op jit(solution)/shard_map/ppermute | solution.py:381
  91.7 2.9 %copy-start.4 = (bf16[2,2,2,2,16,2048]{5,4,3,2,1,0:T(8,128)(2,1)S(1)}, bf16[2,2,2,2,16,2048]{5,4,3,2,1,0:T(8,128)(2,1)}, u32[]{:S(2)}) copy-start(bf16[2,2,2,2,16,2048]{5,4,3,2,1,0:T(8,128)(2,1)} %get-tuple-element.14) | copy-start | bytes 3145732
  177.3 1.6 copy-start.5
  177.4 2.2 %copy-start.3 = (bf16[2,256,1024]{2,1,0:T(8,128)(2,1)S(1)}, bf16[2,256,1024]{2,1,0:T(8,128)(2,1)}, u32[]{:S(2)}) copy-start(bf16[2,256,1024]{2,1,0:T(8,128)(2,1)} %get-tuple-element.22) | copy-start | bytes 3145732
  179.0 5.5 %collective-permute-start.3 = (f32[2,2,8,1024]{3,2,1,0:T(8,128)S(1)}, f32[2,2,8,1024]{3,2,1,0:T(8,128)S(1)}, u32[]{:S(2)}, u32[]{:S(2)}) collective-permute-start(f32[2,2,8,1024]{3,2,1,0:T(8,128)S(1)} %bitcast.139), channel_id=1, source_target_pairs={{0,16},{16,0},{1,17},{17,1},{2,18},{18,2},{3,19},{19,3},{4,20},{20... | collective-permute-start | bytes 393224 | tf_op jit(solution)/shard_map/ppermute | solution.py:400
  180.6 37.5 %collective-permute-start.4 = (bf16[2,128,1024]{2,1,0:T(8,128)(2,1)}, bf16[2,128,1024]{2,1,0:T(8,128)(2,1)}, u32[]{:S(2)}, u32[]{:S(2)}) collective-permute-start(bf16[2,128,1024]{2,1,0:T(8,128)(2,1)} %get-tuple-element.40), channel_id=1, source_target_pairs={{0,1},{1,2},{2,3},{3,4},{4,5},{5,6},{6,7},{7,8},{8,9},{9,10},{10,1... | collective-permute-start | bytes 1572872 | tf_op jit(solution)/shard_map/ppermute | solution.py:388
  180.7 37.5 %collective-permute-start.5 = (bf16[2,128,1024]{2,1,0:T(8,128)(2,1)}, bf16[2,128,1024]{2,1,0:T(8,128)(2,1)}, u32[]{:S(2)}, u32[]{:S(2)}) collective-permute-start(bf16[2,128,1024]{2,1,0:T(8,128)(2,1)} %get-tuple-element.41), channel_id=1, source_target_pairs={{1,0},{2,1},{3,2},{4,3},{5,4},{6,5},{7,6},{8,7},{9,8},{10,9},{11,1... | collective-permute-start | bytes 1572872 | tf_op jit(solution)/shard_map/ppermute | solution.py:387
  218.0 1.6 copy-start.2

commit v5 on v4

--- a/solution.py
+++ b/solution.py
@@ -207,9 +207,8 @@
     return [1 + (cols - 1) * i // levels for i in range(levels + 1)]
 
 
-def late_groups(cols, levels):
-    third, half = 1 + (cols - 1) // 3, 1 + (cols - 1) * 8 // 15
-    return [1, third, third] + [half] * (levels - 3) + [cols] * 1
+def early_groups(cols, levels):
+    return [1] + [cols] * levels
 
 
 def exchange_kernel(cols, from_ref, to_ref, *sems):
@@ -285,7 +284,7 @@
     sems = scratch[2 * levels + 1 :]
     me = lax.axis_index("col")
     greet(me, cols)
-    bounds = late_groups(cols, levels)
+    bounds = early_groups(cols, levels)
     source = parts_ref
     for bit in range(levels):
         dim = levels - 1 - bit

time: 225 us -> 223 us (level)
    pallas_call x1, Pallas kernels: 52.6 us -> 46 us  [reduce_exchange(): pl.pallas_call(functools.partial(reduce_kernel, cols, levels), out_shape=...]
    pallas_call x2, Pallas kernels: 59.1 us -> 64.5 us  [direct_exchange(): pl.pallas_call(functools.partial(exchange_kernel, cols), out_shape=jax.Sh...]
  transfers between devices with their start and end apart: 6 -> 6, of which waited for: 1 -> 0; matrix products, arithmetic and copies ran while one was open for 8% -> 8% of each run, Pallas kernels for 34% -> 37%
where the time goes in v5:
time: 223 us; the launch traced here: 221 us
  Pallas kernels  180 us (81%)
  local copies, waits for them, and re-layouts  25.5 us (11%)
  other arithmetic  9.16 us (4%)
  starting transfers between devices  4.94 us (2%)
    pallas_call x2, Pallas kernels, direct_exchange(): pl.pallas_call(functools.partial(exchange_kernel, cols), out_shape=jax.Sh...  64.5 us
    pallas_call x1, Pallas kernels, reduce_exchange(): pl.pallas_call(functools.partial(reduce_kernel, cols, levels), out_shape=...  46 us
    pallas_call x1, Pallas kernels, gather_exchange(): pl.pallas_call(functools.partial(gather_kernel, cols, levels), out_shape=...  45.1 us
    pallas_call x1, Pallas kernels, attention(): pl.pallas_call(functools.partial(attention_kernel, blocks), grid=(pairs,)...  24.5 us
  transfers between devices with their start and end apart: 6, of which 0 were waited for; matrix products, arithmetic and copies ran while one was open for 8% of the time, Pallas kernels for 37%

profile of v5, /device:TPU:9, one launch (start us, length us, event | category | flops | bytes accessed | tf_op | source)
XLA Modules:
  0.0 220.8 jit_solution(13883228173911205541)
XLA Ops:
  0.6 0.0 copy-start
  0.7 0.7 copy-done
  1.3 0.7 constant_dynamic-slice_fusion.1
  2.0 0.1 select_reduce_fusion.1
  2.1 1.1 constant_dynamic-update-slice_fusion.1
  3.2 1.1 constant_dynamic-update-slice_fusion
  4.3 1.0 copy.58
  5.4 29.0 %direct_exchange.2 = bf16[16,16,2048]{2,1,0:T(8,128)(2,1)} custom-call(bf16[16,16,2048]{2,1,0:T(8,128)(2,1)} %bitcast.136), custom_call_target="tpu_custom_call" | custom-call | flops 30000001024 | bytes 2097152 | tf_op jit(solution)/shard_map/direct_exchange/pallas_call | solution.py:225
  34.3 0.0 copy-start.1
  34.4 1.9 gather_fusion
  36.2 0.1 broadcast_select_fusion
  36.3 1.2 collective-permute-start.2
  37.6 0.9 fusion.13
  38.5 1.2 collective-permute-start
  39.7 0.8 collective-permute-start.1
  40.4 0.6 fusion.14
  41.0 0.1 copy.34
  41.1 0.1 reshape.215
  41.2 0.7 gather_fusion.1
  41.9 0.1 copy.33
  42.0 0.8 copy.37
  42.8 0.1 copy.40
  42.9 0.1 copy.41
  43.0 0.1 copy.38
  43.1 1.3 fusion.8
  44.4 0.1 copy.42
  44.5 0.1 copy.43
  44.6 1.4 bitcast_select_fusion.3.from_ref
  45.9 0.0 collective-permute-done.2
  45.9 0.7 select_bitcast_fusion.strip_ref
  46.6 45.1 %gather_exchange.1 = (bf16[2,2,2,2,16,2048]{5,4,3,2,1,0:T(8,128)(2,1)}, bf16[16,24,2048]{2,1,0:T(8,128)(2,1)}) custom-call(bf16[16,2048]{1,0:T(8,128)(2,1)} %select_bitcast_fusion.strip_ref, bf16[16,24,2048]{2,1,0:T(8,128)(2,1)} %bitcast_select_fusion.3.from_ref), custom_call_target="tpu_custom_call" | custom-call | flops 30000001024 | bytes 3145728 | tf_op jit(solution)/shard_map/gather_exchange/pallas_call | solution.py:265
  91.7 0.0 copy-start.4
  91.7 2.9 %copy.36 = bf16[16,3,8,2048]{3,2,0,1:T(8,128)(2,1)} copy(bf16[16,3,8,2048]{3,2,1,0:T(8,128)(2,1)} %bitcast.129) | data formatting | bytes 3145728 | tf_op jit(solution)/shard_map/reshape | solution.py:377
  94.6 1.1 copy.35
  95.8 0.0 collective-permute-done.kp_ref.vp_ref
  95.8 0.0 collective-permute-done.1.kn_ref.vn_ref
  95.8 24.5 %block_attention.1 = (bf16[256,1024]{1,0:T(8,128)(2,1)}, bf16[256,1024]{1,0:T(8,128)(2,1)}, f32[2,256,1024]{2,1,0:T(8,128)}, bf16[2,256,1024]{2,1,0:T(8,128)(2,1)}, bf16[2,640,1024]{2,1,0:T(8,128)(2,1)}) custom-call(bf16[256,1024]{1,0:T(8,128)(2,1)} %q_ref.1, bf16[256,1024]{1,0:T(8,128)(2,1)} %g_ref.1, bf16[256,1024]{1,0:T(8,128)(2,1)} %ko_ref.1, ...), custom_call_target="tpu_custom_call" | custom-call | flops 3758096384 | bytes 4194304 | tf_op jit(solution)/shard_map/block_attention/pallas_call | solution.py:136
  120.3 2.0 copy.57
  122.3 1.3 slice.99
  123.7 1.1 slice.98
  124.7 46.0 %reduce_exchange.1 = (f32[32,1024]{1,0:T(8,128)}, bf16[16,48,1024]{2,1,0:T(8,128)(2,1)}) custom-call(bf16[2,2,2,2,32,1024]{5,4,3,2,1,0:T(8,128)(2,1)} %bitcast.135, bf16[16,48,1024]{2,1,0:T(8,128)(2,1)} %bitcast.130), custom_call_target="tpu_custom_call" | custom-call | flops 30000001024 | bytes 3145728 | tf_op jit(solution)/shard_map/reduce_exchange/pallas_call | solution.py:321
  170.8 0.0 copy-start.5
  170.8 0.0 copy-start.3
  170.8 1.6 slice_bitcast_fusion.4
  172.4 0.2 collective-permute-start.3
  172.7 1.1 fusion.12
  173.7 1.5 collective-permute-start.4
  175.2 0.0 collective-permute-start.5
  175.2 0.6 gather_fusion.2
  175.8 0.1 select_convert_fusion.2
  176.0 0.6 gather_fusion.4
  176.5 0.1 select_convert_fusion
  176.7 0.6 gather_fusion.3
  177.3 0.1 select_convert_fusion.1
  177.4 0.0 collective-permute-done.3
  177.5 1.8 fusion.6.from_ref
  179.3 35.5 %direct_exchange.3 = bf16[16,32,1024]{2,1,0:T(8,128)(2,1)} custom-call(bf16[16,32,1024]{2,1,0:T(8,128)(2,1)} %fusion.6.from_ref), custom_call_target="tpu_custom_call" | custom-call | flops 30000001024 | bytes 2097152 | tf_op jit(solution)/shard_map/direct_exchange/pallas_call | solution.py:225
  214.9 1.5 convert_bitcast_fusion
  216.4 0.1 copy.44
  216.5 0.0 collective-permute-done.4
  216.5 0.0 collective-permute-done.5
  216.5 1.4 copy-done.2
  217.9 1.8 fusion.2
  219.8 1.0 slice_bitcast_fusion
  (32 shorter events, 0.2 us)
Async XLA Ops:
  0.6 0.7 copy-start
  5.4 29.0 %copy-start.7 = (s32[2]{0:T(128)S(1)}, s32[2]{0:T(128)}, u32[]{:S(2)}) copy-start(s32[2]{0:T(128)} %param.17) | copy-start | bytes 28
  34.3 6.9 %copy-start.1 = (bf16[16,16,2048]{2,1,0:T(8,128)(2,1)S(1)}, bf16[16,16,2048]{2,1,0:T(8,128)(2,1)}, u32[]{:S(2)}) copy-start(bf16[16,16,2048]{2,1,0:T(8,128)(2,1)} %direct_exchange.2) | copy-start | bytes 3145732
  36.3 9.6 %collective-permute-start.2 = (bf16[2,8,2048]{2,1,0:T(8,128)(2,1)S(1)}, bf16[2,8,2048]{2,1,0:T(8,128)(2,1)S(1)}, u32[]{:S(2)}, u32[]{:S(2)}) collective-permute-start(bf16[2,8,2048]{2,1,0:T(8,128)(2,1)S(1)} %broadcast_select_fusion), channel_id=1, source_target_pairs={{0,16},{16,0},{1,17},{17,1},{2,18},{18,2},{3,19},{19,3},{4,20},{20... | collective-permute-start | bytes 196616 | tf_op jit(solution)/shard_map/ppermute | solution.py:370
  38.5 3.5 %copy-start.6 = (s32[256,128]{1,0:T(8,128)S(1)}, s32[256,128]{1,0:T(8,128)}, u32[]{:S(2)}) copy-start(s32[256,128]{1,0:T(8,128)} %param.14) | copy-start | bytes 393220
  38.5 57.3 %collective-permute-start = (bf16[128,2048]{1,0:T(8,128)(2,1)}, bf16[128,2048]{1,0:T(8,128)(2,1)}, u32[]{:S(2)}, u32[]{:S(2)}) collective-permute-start(bf16[128,2048]{1,0:T(8,128)(2,1)} %get-tuple-element.43), channel_id=1, source_target_pairs={{0,1},{1,2},{2,3},{3,4},{4,5},{5,6},{6,7},{7,8},{8,9},{9,10},{10,1... | collective-permute-start | bytes 1572872 | tf_op jit(solution)/shard_map/ppermute | solution.py:379
  39.7 56.1 %collective-permute-start.1 = (bf16[128,2048]{1,0:T(8,128)(2,1)S(1)}, bf16[128,2048]{1,0:T(8,128)(2,1)}, u32[]{:S(2)}, u32[]{:S(2)}) collective-permute-start(bf16[128,2048]{1,0:T(8,128)(2,1)S(1)} %get-tuple-element.42), channel_id=1, source_target_pairs={{1,0},{2,1},{3,2},{4,3},{5,4},{6,5},{7,6},{8,7},{9,8},{10,9},{11,1... | collective-permute-start | bytes 1572872 | tf_op jit(solution)/shard_map/ppermute | solution.py:380
  91.7 2.9 %copy-start.4 = (bf16[2,2,2,2,16,2048]{5,4,3,2,1,0:T(8,128)(2,1)S(1)}, bf16[2,2,2,2,16,2048]{5,4,3,2,1,0:T(8,128)(2,1)}, u32[]{:S(2)}) copy-start(bf16[2,2,2,2,16,2048]{5,4,3,2,1,0:T(8,128)(2,1)} %get-tuple-element.14) | copy-start | bytes 3145732
  170.8 1.6 copy-start.5
  170.8 1.9 copy-start.3
  172.4 5.0 %collective-permute-start.3 = (f32[2,2,8,1024]{3,2,1,0:T(8,128)S(1)}, f32[2,2,8,1024]{3,2,1,0:T(8,128)S(1)}, u32[]{:S(2)}, u32[]{:S(2)}) collective-permute-start(f32[2,2,8,1024]{3,2,1,0:T(8,128)S(1)} %bitcast.139), channel_id=1, source_target_pairs={{0,16},{16,0},{1,17},{17,1},{2,18},{18,2},{3,19},{19,3},{4,20},{20... | collective-permute-start | bytes 393224 | tf_op jit(solution)/shard_map/ppermute | solution.py:399
  173.7 42.8 %collective-permute-start.4 = (bf16[2,128,1024]{2,1,0:T(8,128)(2,1)}, bf16[2,128,1024]{2,1,0:T(8,128)(2,1)}, u32[]{:S(2)}, u32[]{:S(2)}) collective-permute-start(bf16[2,128,1024]{2,1,0:T(8,128)(2,1)} %get-tuple-element.40), channel_id=1, source_target_pairs={{0,1},{1,2},{2,3},{3,4},{4,5},{5,6},{6,7},{7,8},{8,9},{9,10},{10,1... | collective-permute-start | bytes 1572872 | tf_op jit(solution)/shard_map/ppermute | solution.py:387
  175.2 41.3 %collective-permute-start.5 = (bf16[2,128,1024]{2,1,0:T(8,128)(2,1)}, bf16[2,128,1024]{2,1,0:T(8,128)(2,1)}, u32[]{:S(2)}, u32[]{:S(2)}) collective-permute-start(bf16[2,128,1024]{2,1,0:T(8,128)(2,1)} %get-tuple-element.41), channel_id=1, source_target_pairs={{1,0},{2,1},{3,2},{4,3},{5,4},{6,5},{7,6},{8,7},{9,8},{10,9},{11,1... | collective-permute-start | bytes 1572872 | tf_op jit(solution)/shard_map/ppermute | solution.py:386
  216.3 1.6 copy-start.2
